TPU v7x, 32 devices: a whole 2x2x4 slice. The times are simulated.
32 devices in a mesh: gx: 4 (over x, core), gy: 4 (over z), gz: 2 (over y).
Axes of the slice: x: 2, y: 2, z: 4, core: 2. Of those that a mesh axis runs over, the one named last changes fastest.
Arguments:
- wave: float32 [64, 128, 256], P('gx', 'gy', 'gz'), may hold values from -7 to 7
- external: float32 [64, 128, 256], P('gx', 'gy', 'gz'), may hold values from 0 to 2
- weights: float32 [3, 17], replicated, may hold values from 0.02 to 0.1
Outputs:
- wave_next: float32 [64, 128, 256], P('gx', 'gy', 'gz')
- correlation: float32 [64, 128, 256], P('gx', 'gy', 'gz')
All inputs are finite; a program needn't handle non-finite values.
Results may differ from a plain program's by a relative error of at most 0.00029.
Values sent between devices are 32-bit elements; how exact they have to be, the bound alone decides.
A program may use at most 64 MiB of HBM per device.

v0:
```python
import functools

import jax
import jax.numpy as jnp
from jax import lax
from jax.experimental import pallas as pl
from jax.experimental.pallas import tpu as pltpu
from jax.sharding import PartitionSpec as P

SUBSTEPS = 3
LAP_COEF = (-205.0 / 72.0, 8.0 / 5.0, -1.0 / 5.0, 8.0 / 315.0, -1.0 / 560.0)
STEP = 0.08
AXES = ("gx", "gy", "gz")
MESH = pl.DeviceIdType.MESH
R = 8
H = 4


def lanes(shape):
    return lax.broadcasted_iota(jnp.int32, shape, len(shape) - 1)


def lane_taps(mid, low, high, step, taps):
    at = lanes(mid.shape)
    width = mid.shape[-1]
    total = None
    for k, tap in taps:
        if k == 0:
            part = mid
        elif k > 0:
            s = k * step
            part = pltpu.roll(jnp.where(at < s, high, mid), width - s, mid.ndim - 1)
        else:
            s = -k * step
            part = pltpu.roll(jnp.where(at >= width - s, low, mid), s, mid.ndim - 1)
        part = part * tap
        total = part if total is None else total + part
    return total


PARTNERS = [(dx, 0, dz) for dx in (-1, 0, 1) for dz in (-1, 0, 1) if dx or dz] + [(0, 1, 0), (0, -1, 0)]
UNROLL = {"stage": 16, "source": 16, "corr": 16}
ZW = 4


def loop(name, n, body, init):
    width = min(UNROLL[name], n)
    if n % width:
        width = 1
    if width == n:
        for i in range(n):
            init = body(i, init)
        return init

    def step(j, carry):
        for k in range(width):
            carry = body(j * width + k, carry)
        return carry

    return lax.fori_loop(0, n // width, step, init)


def turn(value, shift):
    return value if isinstance(shift, int) and shift == 0 else pltpu.roll(value, shift, 1)


def modulo(a, n):
    return a % n if isinstance(a, int) else lax.rem(a, n)


def kernel(sizes, w_hbm, wave_hbm, ext_hbm, out_ref, corr_ref, scale_ref,
           wb, sb, yb, psi, va, pack, zin, ypack, yin, bands, ext_ref, w_ref, sums, sums2,
           send, recv, send2, recv2, local):
    nx, ny, nz = sizes
    cx, cy, cz = wave_hbm.shape
    wave_ref = wb.at[pl.ds(R, cx), pl.ds(R, cy)]
    get_wave = pltpu.make_async_copy(wave_hbm, wave_ref, local.at[0])
    get_ext = pltpu.make_async_copy(ext_hbm, ext_ref, local.at[1])
    get_weights = pltpu.make_async_copy(w_hbm, w_ref, local.at[2])
    get_wave.start()
    get_weights.start()
    ix, iy, iz = (lax.axis_index(a) for a in AXES)
    plane = nx * nz
    per = cz // cx
    here = ix * nz + iz

    def plane_id(d):
        t = lax.rem(here + d, plane)
        return t, {"gx": lax.div(t, nz), "gz": lax.rem(t, nz)}

    def line_id(d):
        t = lax.rem(iy + d, ny)
        return t, {"gy": t}

    barrier = pltpu.get_barrier_semaphore()

    def greet(ids):
        def body(d, c):
            pl.semaphore_signal(barrier, inc=1, device_id=ids(d)[1], device_id_type=MESH)
            return c
        return body

    near = nx <= 4 and ny <= 4 and nz <= 2
    if near:
        guests = 0
        for dx, dy, dz in PARTNERS:
            there = None
            target = {}
            for name, d, i, n in zip(AXES, (dx, dy, dz), (ix, iy, iz), sizes):
                if d:
                    ok = i < n - 1 if d > 0 else i > 0
                    there = ok if there is None else there & ok
                    target[name] = jnp.clip(i + d, 0, n - 1)
            guests += there.astype(jnp.int32)

            @pl.when(there)
            def _(target=target):
                pl.semaphore_signal(barrier, inc=1, device_id=target, device_id_type=MESH)
    else:
        guests = plane - 1 + ny - 1
        lax.fori_loop(1, plane, greet(plane_id), 0)
        lax.fori_loop(1, ny, greet(line_id), 0)

    counter = [0]

    def message(src, dst, dx, dy, dz):
        k = counter[0]
        counter[0] += 1
        to, back = None, None
        for d, i, n in ((dx, ix, nx), (dy, iy, ny), (dz, iz, nz)):
            if d > 0:
                a, b = i < n - 1, i > 0
            elif d < 0:
                a, b = i > 0, i < n - 1
            else:
                continue
            to = a if to is None else to & a
            back = b if back is None else back & b
        target = {}
        for name, d, i, n in zip(AXES, (dx, dy, dz), (ix, iy, iz), sizes):
            if d:
                target[name] = jnp.clip(i + d, 0, n - 1)
        copy = pltpu.make_async_remote_copy(
            src_ref=src, dst_ref=dst, send_sem=send.at[k], recv_sem=recv.at[k],
            device_id=target, device_id_type=MESH)
        return copy, to, back, dst

    sent = []

    def start(messages):
        for copy, to, _, _ in messages:
            pl.when(to)(copy.start)
            sent.append((copy, to))

    def blank(messages):
        for _, _, back, dst in messages:
            @pl.when(jnp.logical_not(back))
            def _(dst=dst):
                dst[...] = jnp.zeros(dst.shape, dst.dtype)

    def arrive(messages):
        for copy, _, back, _ in messages:
            pl.when(back)(copy.wait_recv)

    at = lanes((cy, cz))
    zero = jnp.zeros((cy, cz), jnp.float32)

    def pack_one(i, value, packs):
        mine = (at >= per * i) & (at < per * i + per)
        low = turn(value, per * i)
        high = turn(value, modulo(per * i + per, cz))
        return jnp.where(mine, low, packs[0]), jnp.where(mine, high, packs[1])

    def unpack(i, from_low, from_high):
        a = turn(from_high, modulo(cz - per * i, cz))
        b = turn(from_low, cz - per - per * i)
        return jnp.where(lanes(a.shape) < per, a, b)

    def pack_out(slot, packs):
        pack[slot, 0] = packs[0]
        pack[slot, 1] = packs[1]

    def z_messages(slot, across):
        out = []
        for dx in ((-1, 0, 1) if across else (0,)):
            out.append(message(pack.at[slot, 1], zin.at[slot, 0, 1 - dx], dx, 0, 1))
            out.append(message(pack.at[slot, 0], zin.at[slot, 1, 1 - dx], dx, 0, -1))
        return out

    def stage(i, packs):
        return pack_one(i, wave_ref[i], packs)

    get_wave.wait()

    pack_out(0, loop("stage", cx, stage, (zero, zero)))

    outer = [(0, R), (cy - R, R)]
    inner = [(R, cy - 2 * R)] if cy > 2 * R else []

    def x_messages(buf, y_at, bands_of_rows):
        out = []
        for first, rows in bands_of_rows:
            rows = pl.ds(y_at + first, rows)
            out.append(message(buf.at[pl.ds(cx, R), rows], buf.at[pl.ds(0, R), rows], 1, 0, 0))
            out.append(message(buf.at[pl.ds(R, R), rows], buf.at[pl.ds(R + cx, R), rows], -1, 0, 0))
        return out

    wave_x, wave_in = x_messages(wb, R, outer), x_messages(wb, R, inner)
    wave_z = z_messages(0, True)
    wave_y = [
        message(wave_ref.at[:, pl.ds(cy - R, R)], wb.at[pl.ds(R, cx), pl.ds(0, R)], 0, 1, 0),
        message(wave_ref.at[:, pl.ds(0, R)], wb.at[pl.ds(R, cx), pl.ds(R + cy, R)], 0, -1, 0),
    ]

    def y_messages(buf):
        return [
            message(buf.at[:, pl.ds(cy, R)], buf.at[:, pl.ds(0, R)], 0, 1, 0),
            message(buf.at[:, pl.ds(R, R)], buf.at[:, pl.ds(R + cy, R)], 0, -1, 0),
        ]

    mid_y = y_messages(yb.at[0])
    src_x, src_in = x_messages(sb, 0, outer), x_messages(sb, 0, inner)
    src_z = z_messages(1, True)
    end_y = y_messages(yb.at[1])

    psi_moves = []
    for s in range(SUBSTEPS - 1):
        buf = psi.at[s]
        moves = [
            message(buf.at[pl.ds(cx, H), pl.ds(R, cy)], buf.at[pl.ds(0, H), pl.ds(R, cy)], 1, 0, 0),
            message(buf.at[pl.ds(H, H), pl.ds(R, cy)], buf.at[pl.ds(H + cx, H), pl.ds(R, cy)], -1, 0, 0),
        ]
        moves += [
            message(ypack.at[s, 1], yin.at[s, 0], 0, 1, 0),
            message(ypack.at[s, 0], yin.at[s, 1], 0, -1, 0),
        ]
        moves += z_messages(2 + s, False)
        psi_moves.append(moves)

    pl.semaphore_wait(barrier, guests)
    start(wave_x + wave_z + wave_in + wave_y)
    get_ext.start()
    get_weights.wait()
    for group in [wave_x, wave_in, wave_z, wave_y, mid_y, src_x, src_in, src_z, end_y] + psi_moves:
        blank(group)

    def taps_of(dim, flip):
        return [(k, w_ref[dim, R - k if flip else R + k]) for k in range(-R, R + 1)]

    row = lax.broadcasted_iota(jnp.int32, (cz, cz), 0)
    gap = row - lanes((cz, cz))

    def band(slot, taps):
        inner = jnp.zeros((cz, cz), jnp.float32)
        outer = inner
        for k, tap in taps:
            inner = jnp.where(gap == k, tap, inner)
            if k:
                outer = jnp.where(gap == (k - cz if k > 0 else k + cz), tap, outer)
        bands[slot, pl.ds(0, cz)] = inner
        bands[slot, pl.ds(cz, cz)] = outer

    def along_z(values, nears, slot):
        both = jnp.concatenate([jnp.concatenate(values, 0), jnp.concatenate(nears, 0)], 1)
        return jnp.dot(both, bands[slot], precision=lax.Precision.HIGHEST,
                       preferred_element_type=jnp.float32)

    band(0, taps_of(2, False))
    band(1, taps_of(2, True))
    gains = [STEP * 0.5 * c for c in LAP_COEF]
    band(2, [(k, gains[abs(k)]) for k in range(-H, H + 1) if k])

    def smear_xz(src, y_at, slot, square, flip, buf, late, leave):
        taps = taps_of(0, flip)
        sides = []
        for side in range(2):
            near = [zin[slot, side, place] for place in range(3)]
            if square:
                near = [v * v for v in near]
            sides.append(lane_taps(near[1], near[0], near[2], per, taps))

        def tile(first):
            ins = [src[k, pl.ds(y_at + first, 8)] for k in range(cx + 2 * R)]
            if square:
                ins = [v * v for v in ins]
            outs = []
            for i in range(cx):
                total = None
                for k, tap in taps:
                    part = ins[i + R + k] * tap
                    total = part if total is None else total + part
                outs.append(total)
            below, above = (v[first:first + 8] for v in sides)
            made = along_z(outs, [unpack(i, below, above) for i in range(cx)], int(flip))
            for i in range(cx):
                buf[i, pl.ds(R + first, 8)] = made[8 * i:8 * i + 8]

        for first, rows in outer:
            for f in range(first, first + rows, 8):
                tile(f)
        start(leave)
        arrive(late)
        for first, rows in inner:
            for f in range(first, first + rows, 8):
                tile(f)
        arrive(leave)

    def smear_y(buf, i, taps):
        total = None
        for k, tap in taps:
            part = buf[i, pl.ds(R + k, cy)] * tap
            total = part if total is None else total + part
        return total

    arrive(wave_x + wave_z)
    smear_xz(wb, R, 0, True, False, yb.at[0], wave_in, mid_y)
    taps_y = taps_of(1, False)

    def source_pass(i, packs):
        coarse = smear_y(yb.at[0], i, taps_y)
        value = wave_ref[i]
        dens = value * value
        both = coarse * coarse
        source = 0.5 * dens * both - dens * coarse
        corr_ref[i] = (0.5 / 3.0) * both * coarse - 0.5 * both
        sb[R + i] = source
        return pack_one(i, source, packs)

    pack_out(1, loop("source", cx, source_pass, (zero, zero)))

    start(src_x + src_z + src_in)
    arrive(src_x + src_z)
    smear_xz(sb, 0, 1, False, True, yb.at[1], src_in, end_y)
    taps_yt = taps_of(1, True)

    get_ext.wait()

    def corr_pass(i, c):
        corr = corr_ref[i] + smear_y(yb.at[1], i, taps_yt)
        corr_ref[i] = corr
        va[i] = (1.0 + STEP * 0.5 * 3.0 * LAP_COEF[0]) - STEP * (corr + ext_ref[i])
        return c

    loop("corr", cx, corr_pass, 0)


    def advance(buf, reach, these, below, above):
        centers = [buf[reach + i, pl.ds(R, cy)] for i in these]
        along = along_z(centers, [unpack(i, below, above) for i in these], 2)
        made = []
        for at_, i in enumerate(these):
            total = centers[at_] * va[i] + along[at_ * cy:(at_ + 1) * cy]
            for k in range(1, H + 1):
                pair = buf[reach + i + k, pl.ds(R, cy)] + buf[reach + i - k, pl.ds(R, cy)]
                pair += buf[reach + i, pl.ds(R + k, cy)] + buf[reach + i, pl.ds(R - k, cy)]
                total += gains[k] * pair
            made.append(total)
        return made

    groups = [list(range(g, g + ZW)) for g in range(0, cx, ZW)]
    groups = groups[:1] + groups[-1:] + groups[1:-1]
    arrive(wave_y)
    buf, reach, slot = wb, R, 0
    for s in range(SUBSTEPS):
        if s:
            arrive(psi_moves[s - 1])
            for i in range(cx):
                half = pl.ds(H * (i % 2), H)
                buf[H + i, pl.ds(R - H, H)] = yin[s - 1, 0, i // 2, half]
                buf[H + i, pl.ds(R + cy, H)] = yin[s - 1, 1, i // 2, half]
        below, above = zin[slot, 0, 1], zin[slot, 1, 1]
        if s < SUBSTEPS - 1:
            after = psi.at[s]
            packs = (zero, zero)
            for n_, these in enumerate(groups):
                for i, value in zip(these, advance(buf, reach, these, below, above)):
                    after[H + i, pl.ds(R, cy)] = value
                    packs = pack_one(i, value, packs)
                    half = pl.ds(H * (i % 2), H)
                    ypack[s, 0, i // 2, half] = value[:H]
                    ypack[s, 1, i // 2, half] = value[cy - H:]
                if n_ == 1:
                    start(psi_moves[s][:2])
            pack_out(2 + s, packs)
            start(psi_moves[s][2:])
            buf, reach, slot = after, H, 2 + s
        else:
            total = zero
            for these in groups:
                for i, value in zip(these, advance(buf, reach, these, below, above)):
                    out_ref[i] = value
                    total = total + value * value

    part = jnp.sum(total, axis=0, keepdims=True)
    everyone = plane * ny
    me = iy * plane + here

    def any_id(d):
        t = lax.rem(me + d, everyone)
        p = lax.rem(t, plane)
        return t, {"gx": lax.div(p, nz), "gy": lax.div(t, plane), "gz": lax.rem(p, nz)}

    def all_sum(part, slots, ssem, rsem, me, n, ids):
        if n == 1:
            return part
        slots[me] = part

        def copy_of(d, slot):
            return pltpu.make_async_remote_copy(
                src_ref=slots.at[me], dst_ref=slots.at[slot], send_sem=ssem.at[d], recv_sem=rsem.at[slot],
                device_id=ids(d)[1], device_id_type=MESH)

        def go(d, c):
            copy_of(d, me).start()
            return c

        def come(d, c):
            copy_of(d, ids(d)[0]).wait_recv()
            return c

        def left(d, c):
            copy_of(d, me).wait_send()
            return c

        lax.fori_loop(1, n, go, 0)
        lax.fori_loop(1, n, come, 0)
        total = jnp.sum(slots[...], axis=0)
        lax.fori_loop(1, n, left, 0)
        return total

    if near:
        part = all_sum(part, sums, send2.at[0], recv2.at[0], me, everyone, any_id)
    else:
        part = all_sum(part, sums, send2.at[0], recv2.at[0], here, plane, plane_id)
        part = all_sum(part, sums2, send2.at[1], recv2.at[1], iy, ny, line_id)
    cells = float(cx * cy * cz * nx * ny * nz)
    scale_ref[...] = lax.rsqrt(jnp.full(scale_ref.shape, jnp.sum(part), jnp.float32) / cells + 1e-06)
    for copy, to in sent:
        pl.when(to)(copy.wait_send)


def shards(sizes, wave, external, weights):
    cx, cy, cz = wave.shape
    nx, ny, nz = sizes
    f32 = jnp.float32
    n_messages = 44
    summed = nx * ny * nz if nx <= 4 and ny <= 4 and nz <= 2 else nx * nz
    most = max(summed, ny)
    vmem = pl.BlockSpec(memory_space=pltpu.VMEM)
    stay = pl.BlockSpec(memory_space=pltpu.HBM)
    psi, corr, scale = pl.pallas_call(
        functools.partial(kernel, sizes),
        out_shape=(jax.ShapeDtypeStruct(wave.shape, f32), jax.ShapeDtypeStruct(wave.shape, f32),
                   jax.ShapeDtypeStruct((8, cz), f32)),
        in_specs=[stay, stay, stay],
        out_specs=(vmem, vmem, vmem),
        scratch_shapes=[
            pltpu.VMEM((cx + 2 * R, cy + 2 * R, cz), f32),
            pltpu.VMEM((cx + 2 * R, cy, cz), f32),
            pltpu.VMEM((2, cx, cy + 2 * R, cz), f32),
            pltpu.VMEM((SUBSTEPS - 1, cx + 2 * H, cy + 2 * R, cz), f32),
            pltpu.VMEM((cx, cy, cz), f32),
            pltpu.VMEM((SUBSTEPS + 1, 2, cy, cz), f32),
            pltpu.VMEM((SUBSTEPS + 1, 2, 3, cy, cz), f32),
            pltpu.VMEM((SUBSTEPS - 1, 2, cx // 2, 2 * H, cz), f32),
            pltpu.VMEM((SUBSTEPS - 1, 2, cx // 2, 2 * H, cz), f32),
            pltpu.VMEM((3, 2 * cz, cz), f32),
            pltpu.VMEM((cx, cy, cz), f32),
            pltpu.SMEM(weights.shape, f32),
            pltpu.VMEM((summed, 1, cz), f32),
            pltpu.VMEM((ny, 1, cz), f32),
            pltpu.SemaphoreType.DMA((n_messages,)),
            pltpu.SemaphoreType.DMA((n_messages,)),
            pltpu.SemaphoreType.DMA((2, most)),
            pltpu.SemaphoreType.DMA((2, most)),
            pltpu.SemaphoreType.DMA((3,)),
        ],
        compiler_params=pltpu.CompilerParams(collective_id=0, has_side_effects=True,
                                             vmem_limit_bytes=48 * 1024 * 1024),
    )(*[pltpu.with_memory_space_constraint(x, pltpu.HBM) for x in (weights, wave, external)])
    return psi * scale[0, 0], corr


def solution(mesh):
    sizes = tuple(mesh.shape[a] for a in AXES)
    spec = P(*AXES)
    return jax.shard_map(
        functools.partial(shards, sizes),
        mesh=mesh,
        in_specs=(spec, spec, P()),
        out_specs=(spec, spec),
        check_vma=False,
    )
```

profile of v0, /device:TPU:0, one launch (start us, length us, event | category | flops | bytes accessed | tf_op | source)
XLA Modules:
  0.0 39.0 jit_solution(14778226775452915644)
XLA Ops:
  0.6 35.8 %shard_map.50 = (f32[16,32,128]{2,1,0:T(8,128)S(1)}, f32[16,32,128]{2,1,0:T(8,128)S(1)}, f32[8,128]{1,0:T(8,128)S(1)}) custom-call(f32[3,17]{1,0:T(4,128)} %w_hbm.1, f32[16,32,128]{2,1,0:T(8,128)} %wave_hbm.1, f32[16,32,128]{2,1,0:T(8,128)} %ext_hbm.1), custom_call_target="tpu_custom_call" | custom-call | tf_op jit(solution)/shard_map/pallas_call | solution.py:451
  36.5 0.5 %slice.3 = f32[1,1]{1,0:T(1,128)} slice(f32[8,128]{1,0:T(8,128)S(1)} %get-tuple-element.6), slice={[0:1], [0:1]} | slice | bytes 8 | tf_op jit(solution)/shard_map/slice | solution.py:481
  37.0 1.4 %broadcast_multiply_fusion = f32[16,32,128]{2,1,0:T(8,128)} fusion(f32[16,32,128]{2,1,0:T(8,128)S(1)} %get-tuple-element.5, f32[]{:T(128)} %bitcast), kind=kLoop, calls=%fused_computation | loop fusion | flops 65536 | bytes 524292 | tf_op jit(solution)/shard_map/mul | solution.py:481
  38.3 0.7 %copy.6 = f32[16,32,128]{2,1,0:T(8,128)} copy(f32[16,32,128]{2,1,0:T(8,128)S(1)} %get-tuple-element.11) | data formatting | bytes 524288
where the time goes:
time: 39.2 us; the launch traced here: 39 us
  Pallas kernels  35.8 us (91%)
  other arithmetic  1.37 us (3%)
  local copies, waits for them, and re-layouts  1.22 us (3%)
  between operations  0.64 us (2%)
    pallas_call x1, Pallas kernels, shards(): pl.pallas_call(functools.partial(kernel, sizes), out_shape=(jax.ShapeDtyp...  35.8 us
    mul x1, other arithmetic, shards(): return (psi * scale[0, 0], corr)  1.37 us

commit v1 on v0

--- a/solution.py
+++ b/solution.py
@@ -38,7 +38,7 @@
     return total
 
 
-PARTNERS = [(dx, 0, dz) for dx in (-1, 0, 1) for dz in (-1, 0, 1) if dx or dz] + [(0, 1, 0), (0, -1, 0)]
+FACES = [(1, 0, 0), (-1, 0, 0), (0, 1, 0), (0, -1, 0), (0, 0, 1), (0, 0, -1)]
 UNROLL = {"stage": 16, "source": 16, "corr": 16}
 ZW = 4
 
@@ -70,7 +70,7 @@
 
 def kernel(sizes, w_hbm, wave_hbm, ext_hbm, out_ref, corr_ref, scale_ref,
            wb, sb, yb, psi, va, pack, zin, ypack, yin, bands, ext_ref, w_ref, sums, sums2,
-           send, recv, send2, recv2, local):
+           send, recv, send2, recv2, local, known):
     nx, ny, nz = sizes
     cx, cy, cz = wave_hbm.shape
     wave_ref = wb.at[pl.ds(R, cx), pl.ds(R, cy)]
@@ -101,21 +101,23 @@
         return body
 
     near = nx <= 4 and ny <= 4 and nz <= 2
-    if near:
-        guests = 0
-        for dx, dy, dz in PARTNERS:
-            there = None
-            target = {}
-            for name, d, i, n in zip(AXES, (dx, dy, dz), (ix, iy, iz), sizes):
+
+    def greet_faces(sem):
+        count = 0
+        for d3 in FACES:
+            for name, d, i, n in zip(AXES, d3, (ix, iy, iz), sizes):
                 if d:
-                    ok = i < n - 1 if d > 0 else i > 0
-                    there = ok if there is None else there & ok
-                    target[name] = jnp.clip(i + d, 0, n - 1)
-            guests += there.astype(jnp.int32)
+                    there = i < n - 1 if d > 0 else i > 0
+                    target = {name: jnp.clip(i + d, 0, n - 1)}
+            count += there.astype(jnp.int32)
 
             @pl.when(there)
             def _(target=target):
-                pl.semaphore_signal(barrier, inc=1, device_id=target, device_id_type=MESH)
+                pl.semaphore_signal(sem, inc=1, device_id=target, device_id_type=MESH)
+        return count
+
+    if near:
+        guests = greet_faces(barrier)
     else:
         guests = plane - 1 + ny - 1
         lax.fori_loop(1, plane, greet(plane_id), 0)
@@ -180,48 +182,67 @@
         pack[slot, 0] = packs[0]
         pack[slot, 1] = packs[1]
 
-    def z_messages(slot, across):
+    def z_messages(slot, dxs, dys):
         out = []
-        for dx in ((-1, 0, 1) if across else (0,)):
-            out.append(message(pack.at[slot, 1], zin.at[slot, 0, 1 - dx], dx, 0, 1))
-            out.append(message(pack.at[slot, 0], zin.at[slot, 1, 1 - dx], dx, 0, -1))
+        for dx in dxs:
+            for dy in dys:
+                if dy > 0:
+                    rows, into = pl.ds(cy - R, R), pl.ds(0, R)
+                elif dy < 0:
+                    rows, into = pl.ds(0, R), pl.ds(R + cy, R)
+                else:
+                    rows, into = pl.ds(0, cy), pl.ds(R, cy)
+                out.append(message(pack.at[slot, 1, rows], zin.at[slot, 0, 1 - dx, into], dx, dy, 1))
+                out.append(message(pack.at[slot, 0, rows], zin.at[slot, 1, 1 - dx, into], dx, dy, -1))
         return out
 
     def stage(i, packs):
         return pack_one(i, wave_ref[i], packs)
 
+    half = cy // 2
+    halves = [(0, half), (half, half)] if half % 8 == 0 else [(0, cy)]
+
+    def side_messages(src, dst, moves):
+        out = []
+        for dx, dy, first, rows in moves:
+            if dx > 0:
+                sx, tx = pl.ds(cx - R, R), pl.ds(0, R)
+            elif dx < 0:
+                sx, tx = pl.ds(0, R), pl.ds(R + cx, R)
+            else:
+                sx, tx = pl.ds(0, cx), pl.ds(R, cx)
+            if dy > 0:
+                sy, ty = pl.ds(cy - R, R), pl.ds(0, R)
+            elif dy < 0:
+                sy, ty = pl.ds(0, R), pl.ds(R + cy, R)
+            else:
+                sy, ty = pl.ds(first, rows), pl.ds(R + first, rows)
+            out.append(message(src.at[sx, sy], dst.at[tx, ty], dx, dy, 0))
+        return out
+
+    face_x = [(dx, 0, first, rows) for first, rows in halves for dx in (1, -1)]
+    face_y = [(0, dy, 0, 0) for dy in (1, -1)]
+    edge_xy = [(dx, dy, 0, 0) for dx in (1, -1) for dy in (1, -1)]
+    src_ref = sb.at[pl.ds(R, cx), pl.ds(R, cy)]
+    wave_x, wave_y, wave_xy = (side_messages(wave_hbm, wb, m) for m in (face_x, face_y, edge_xy))
+    wave_z, wave_xz = z_messages(0, (0,), (0,)), z_messages(0, (-1, 1), (0,))
+    wave_yz, wave_xyz = z_messages(0, (0,), (-1, 1)), z_messages(0, (-1, 1), (-1, 1))
+    src_x, src_y, src_xy = (side_messages(src_ref, sb, m) for m in (face_x, face_y, edge_xy))
+    src_z, src_e = z_messages(1, (-1, 0, 1), (0,)), z_messages(1, (-1, 0, 1), (-1, 1))
+
+    pl.semaphore_wait(barrier, guests)
+    start(wave_x + wave_y)
+    mates = greet_faces(known.at[0])
     get_wave.wait()
 
     pack_out(0, loop("stage", cx, stage, (zero, zero)))
 
-    outer = [(0, R), (cy - R, R)]
-    inner = [(R, cy - 2 * R)] if cy > 2 * R else []
-
-    def x_messages(buf, y_at, bands_of_rows):
-        out = []
-        for first, rows in bands_of_rows:
-            rows = pl.ds(y_at + first, rows)
-            out.append(message(buf.at[pl.ds(cx, R), rows], buf.at[pl.ds(0, R), rows], 1, 0, 0))
-            out.append(message(buf.at[pl.ds(R, R), rows], buf.at[pl.ds(R + cx, R), rows], -1, 0, 0))
-        return out
-
-    wave_x, wave_in = x_messages(wb, R, outer), x_messages(wb, R, inner)
-    wave_z = z_messages(0, True)
-    wave_y = [
-        message(wave_ref.at[:, pl.ds(cy - R, R)], wb.at[pl.ds(R, cx), pl.ds(0, R)], 0, 1, 0),
-        message(wave_ref.at[:, pl.ds(0, R)], wb.at[pl.ds(R, cx), pl.ds(R + cy, R)], 0, -1, 0),
-    ]
-
-    def y_messages(buf):
-        return [
-            message(buf.at[:, pl.ds(cy, R)], buf.at[:, pl.ds(0, R)], 0, 1, 0),
-            message(buf.at[:, pl.ds(R, R)], buf.at[:, pl.ds(R + cy, R)], 0, -1, 0),
-        ]
-
-    mid_y = y_messages(yb.at[0])
-    src_x, src_in = x_messages(sb, 0, outer), x_messages(sb, 0, inner)
-    src_z = z_messages(1, True)
-    end_y = y_messages(yb.at[1])
+    start(wave_z)
+    pl.semaphore_wait(known.at[0], mates)
+    greet_faces(known.at[1])
+    start(wave_xz + wave_xy + wave_yz)
+    get_ext.start()
+    get_weights.wait()
 
     psi_moves = []
     for s in range(SUBSTEPS - 1):
@@ -234,14 +255,11 @@
             message(ypack.at[s, 1], yin.at[s, 0], 0, 1, 0),
             message(ypack.at[s, 0], yin.at[s, 1], 0, -1, 0),
         ]
-        moves += z_messages(2 + s, False)
+        moves += z_messages(2 + s, (0,), (0,))
         psi_moves.append(moves)
 
-    pl.semaphore_wait(barrier, guests)
-    start(wave_x + wave_z + wave_in + wave_y)
-    get_ext.start()
-    get_weights.wait()
-    for group in [wave_x, wave_in, wave_z, wave_y, mid_y, src_x, src_in, src_z, end_y] + psi_moves:
+    for group in [wave_x, wave_y, wave_xy, wave_z, wave_xz, wave_yz, wave_xyz,
+                  src_x, src_y, src_xy, src_z, src_e] + psi_moves:
         blank(group)
 
     def taps_of(dim, flip):
@@ -270,17 +288,17 @@
     gains = [STEP * 0.5 * c for c in LAP_COEF]
     band(2, [(k, gains[abs(k)]) for k in range(-H, H + 1) if k])
 
-    def smear_xz(src, y_at, slot, square, flip, buf, late, leave):
+    def smear_xz(src, slot, square, flip, buf, first_wait, late_wait):
         taps = taps_of(0, flip)
-        sides = []
-        for side in range(2):
-            near = [zin[slot, side, place] for place in range(3)]
-            if square:
-                near = [v * v for v in near]
-            sides.append(lane_taps(near[1], near[0], near[2], per, taps))
 
         def tile(first):
-            ins = [src[k, pl.ds(y_at + first, 8)] for k in range(cx + 2 * R)]
+            sides = []
+            for side in range(2):
+                near = [zin[slot, side, place, pl.ds(R + first, 8)] for place in range(3)]
+                if square:
+                    near = [v * v for v in near]
+                sides.append(lane_taps(near[1], near[0], near[2], per, taps))
+            ins = [src[k, pl.ds(R + first, 8)] for k in range(cx + 2 * R)]
             if square:
                 ins = [v * v for v in ins]
             outs = []
@@ -290,20 +308,17 @@
                     part = ins[i + R + k] * tap
                     total = part if total is None else total + part
                 outs.append(total)
-            below, above = (v[first:first + 8] for v in sides)
-            made = along_z(outs, [unpack(i, below, above) for i in range(cx)], int(flip))
+            made = along_z(outs, [unpack(i, *sides) for i in range(cx)], int(flip))
             for i in range(cx):
                 buf[i, pl.ds(R + first, 8)] = made[8 * i:8 * i + 8]
 
-        for first, rows in outer:
+        for (first, rows), wait in zip(halves, first_wait):
+            arrive(wait)
             for f in range(first, first + rows, 8):
                 tile(f)
-        start(leave)
-        arrive(late)
-        for first, rows in inner:
-            for f in range(first, first + rows, 8):
-                tile(f)
-        arrive(leave)
+        arrive(late_wait)
+        tile(-8)
+        tile(cy)
 
     def smear_y(buf, i, taps):
         total = None
@@ -312,8 +327,15 @@
             total = part if total is None else total + part
         return total
 
-    arrive(wave_x + wave_z)
-    smear_xz(wb, R, 0, True, False, yb.at[0], wave_in, mid_y)
+    pl.semaphore_wait(known.at[1], mates)
+    start(wave_xyz)
+
+    def in_turn(faces, packs):
+        each = [faces[2 * n:2 * n + 2] for n in range(len(halves))]
+        each[0] = packs + each[0]
+        return each
+
+    smear_xz(wb, 0, True, False, yb.at[0], in_turn(wave_x, wave_z + wave_xz), wave_y + wave_xy + wave_yz + wave_xyz)
     taps_y = taps_of(1, False)
 
     def source_pass(i, packs):
@@ -323,14 +345,13 @@
         both = coarse * coarse
         source = 0.5 * dens * both - dens * coarse
         corr_ref[i] = (0.5 / 3.0) * both * coarse - 0.5 * both
-        sb[R + i] = source
+        sb[R + i, pl.ds(R, cy)] = source
         return pack_one(i, source, packs)
 
     pack_out(1, loop("source", cx, source_pass, (zero, zero)))
 
-    start(src_x + src_z + src_in)
-    arrive(src_x + src_z)
-    smear_xz(sb, 0, 1, False, True, yb.at[1], src_in, end_y)
+    start(src_x + src_z + src_e + src_xy + src_y)
+    smear_xz(sb, 1, False, True, yb.at[1], in_turn(src_x, src_z), src_y + src_xy + src_e)
     taps_yt = taps_of(1, True)
 
     get_ext.wait()
@@ -359,7 +380,6 @@
 
     groups = [list(range(g, g + ZW)) for g in range(0, cx, ZW)]
     groups = groups[:1] + groups[-1:] + groups[1:-1]
-    arrive(wave_y)
     buf, reach, slot = wb, R, 0
     for s in range(SUBSTEPS):
         if s:
@@ -368,7 +388,7 @@
                 half = pl.ds(H * (i % 2), H)
                 buf[H + i, pl.ds(R - H, H)] = yin[s - 1, 0, i // 2, half]
                 buf[H + i, pl.ds(R + cy, H)] = yin[s - 1, 1, i // 2, half]
-        below, above = zin[slot, 0, 1], zin[slot, 1, 1]
+        below, above = (zin[slot, side, 1, pl.ds(R, cy)] for side in range(2))
         if s < SUBSTEPS - 1:
             after = psi.at[s]
             packs = (zero, zero)
@@ -429,7 +449,17 @@
         return total
 
     if near:
-        part = all_sum(part, sums, send2.at[0], recv2.at[0], me, everyone, any_id)
+        sums[0] = part
+        for d in range(1, everyone):
+            pltpu.make_async_remote_copy(
+                src_ref=sums.at[0], dst_ref=sums.at[d], send_sem=send2.at[0, 0], recv_sem=recv2.at[0, 0],
+                device_id=any_id(d)[1], device_id_type=MESH).start()
+        rest = sums.at[pl.ds(1, everyone - 1)]
+        whole = pltpu.make_async_remote_copy(
+            src_ref=rest, dst_ref=rest, send_sem=send2.at[0, 0], recv_sem=recv2.at[0, 0],
+            device_id=any_id(1)[1], device_id_type=MESH)
+        whole.wait_recv()
+        part = jnp.sum(sums[...], axis=0)
     else:
         part = all_sum(part, sums, send2.at[0], recv2.at[0], here, plane, plane_id)
         part = all_sum(part, sums2, send2.at[1], recv2.at[1], iy, ny, line_id)
@@ -437,13 +467,30 @@
     scale_ref[...] = lax.rsqrt(jnp.full(scale_ref.shape, jnp.sum(part), jnp.float32) / cells + 1e-06)
     for copy, to in sent:
         pl.when(to)(copy.wait_send)
+    if near:
+        whole.wait_send()
+
+
+def finish(psi_ref, corr_ref, scale_ref, out_hbm, corr_hbm, scaled, sems):
+    copies = [pltpu.make_async_copy(corr_ref, corr_hbm, sems.at[0])]
+    copies[0].start()
+    cx, cy, cz = psi_ref.shape
+    scale = scale_ref[0:1]
+    steps = 2 if cx % 2 == 0 else 1
+    for n in range(steps):
+        some = pl.ds(n * (cx // steps), cx // steps)
+        scaled[some] = psi_ref[some] * scale.reshape(1, 1, cz)
+        copies.append(pltpu.make_async_copy(scaled.at[some], out_hbm.at[some], sems.at[1 + n]))
+        copies[-1].start()
+    for copy in copies:
+        copy.wait()
 
 
 def shards(sizes, wave, external, weights):
     cx, cy, cz = wave.shape
     nx, ny, nz = sizes
     f32 = jnp.float32
-    n_messages = 44
+    n_messages = 72
     summed = nx * ny * nz if nx <= 4 and ny <= 4 and nz <= 2 else nx * nz
     most = max(summed, ny)
     vmem = pl.BlockSpec(memory_space=pltpu.VMEM)
@@ -456,12 +503,12 @@
         out_specs=(vmem, vmem, vmem),
         scratch_shapes=[
             pltpu.VMEM((cx + 2 * R, cy + 2 * R, cz), f32),
-            pltpu.VMEM((cx + 2 * R, cy, cz), f32),
+            pltpu.VMEM((cx + 2 * R, cy + 2 * R, cz), f32),
             pltpu.VMEM((2, cx, cy + 2 * R, cz), f32),
             pltpu.VMEM((SUBSTEPS - 1, cx + 2 * H, cy + 2 * R, cz), f32),
             pltpu.VMEM((cx, cy, cz), f32),
             pltpu.VMEM((SUBSTEPS + 1, 2, cy, cz), f32),
-            pltpu.VMEM((SUBSTEPS + 1, 2, 3, cy, cz), f32),
+            pltpu.VMEM((SUBSTEPS + 1, 2, 3, cy + 2 * R, cz), f32),
             pltpu.VMEM((SUBSTEPS - 1, 2, cx // 2, 2 * H, cz), f32),
             pltpu.VMEM((SUBSTEPS - 1, 2, cx // 2, 2 * H, cz), f32),
             pltpu.VMEM((3, 2 * cz, cz), f32),
@@ -474,11 +521,18 @@
             pltpu.SemaphoreType.DMA((2, most)),
             pltpu.SemaphoreType.DMA((2, most)),
             pltpu.SemaphoreType.DMA((3,)),
+            pltpu.SemaphoreType.REGULAR((2,)),
         ],
         compiler_params=pltpu.CompilerParams(collective_id=0, has_side_effects=True,
                                              vmem_limit_bytes=48 * 1024 * 1024),
     )(*[pltpu.with_memory_space_constraint(x, pltpu.HBM) for x in (weights, wave, external)])
-    return psi * scale[0, 0], corr
+    return pl.pallas_call(
+        finish,
+        out_shape=(jax.ShapeDtypeStruct(wave.shape, f32), jax.ShapeDtypeStruct(wave.shape, f32)),
+        in_specs=[vmem, vmem, vmem],
+        out_specs=(stay, stay),
+        scratch_shapes=[pltpu.VMEM((cx, cy, cz), f32), pltpu.SemaphoreType.DMA((3,))],
+    )(psi, corr, scale)
 
 
 def solution(mesh):

time: 39.2 us -> 39 us (level)
  other arithmetic: 1.37 us -> 0 us
  local copies, waits for them, and re-layouts: 1.22 us -> 1.97 us
  Pallas kernels: 35.8 us -> 36.3 us
    pallas_call x0 -> x1, Pallas kernels: none -> 1.84 us  [shards(): pl.pallas_call(finish, out_shape=(jax.ShapeDtypeStruct(wave.shape, f32),...]
    pallas_call x1, Pallas kernels: 35.8 us -> 34.4 us  [shards(): pl.pallas_call(functools.partial(kernel, sizes), out_shape=(jax.ShapeDtyp...]
    mul x1 -> x0, other arithmetic: 1.37 us -> none  [shards(): return (psi * scale[0, 0], corr)]
    unnamed x1 -> x6, local copies, waits for them, and re-layouts: 0.7 us -> 1.97 us
    slice x1 -> x0, local copies, waits for them, and re-layouts: 0.51 us -> none  [shards(): return (psi * scale[0, 0], corr)]
where the time goes in v1:
time: 39 us; the launch traced here: 38.9 us
  Pallas kernels  36.3 us (93%)
  local copies, waits for them, and re-layouts  1.97 us (5%)
  between operations  0.65 us (2%)
    pallas_call x1, Pallas kernels, shards(): pl.pallas_call(functools.partial(kernel, sizes), out_shape=(jax.ShapeDtyp...  34.4 us
    unnamed x6, local copies, waits for them, and re-layouts  1.97 us
    pallas_call x1, Pallas kernels, shards(): pl.pallas_call(finish, out_shape=(jax.ShapeDtypeStruct(wave.shape, f32),...  1.84 us

profile of v1, /device:TPU:0, one launch (start us, length us, event | category | flops | bytes accessed | tf_op | source)
XLA Modules:
  0.0 38.9 jit_solution(10997797856238831148)
XLA Ops:
  0.6 34.4 %shard_map.50 = (f32[16,32,128]{2,1,0:T(8,128)S(1)}, f32[16,32,128]{2,1,0:T(8,128)S(1)}, f32[8,128]{1,0:T(8,128)S(1)}) custom-call(f32[3,17]{1,0:T(4,128)} %w_hbm.1, f32[16,32,128]{2,1,0:T(8,128)} %wave_hbm.1, f32[16,32,128]{2,1,0:T(8,128)} %ext_hbm.1), custom_call_target="tpu_custom_call" | custom-call | tf_op jit(solution)/shard_map/pallas_call | solution.py:498
  35.1 0.0 copy-start
  35.1 0.7 %copy-done = f32[16,32,128]{2,1,0:T(8,128)} copy-done((f32[16,32,128]{2,1,0:T(8,128)}, f32[16,32,128]{2,1,0:T(8,128)S(1)}, u32[]{:S(2)}) %copy-start) | copy-done | bytes 262168
  35.8 0.0 copy-start.1
  35.8 0.7 %copy-done.1 = f32[16,32,128]{2,1,0:T(8,128)} copy-done((f32[16,32,128]{2,1,0:T(8,128)}, f32[16,32,128]{2,1,0:T(8,128)S(1)}, u32[]{:S(2)}) %copy-start.1) | copy-done | bytes 262168
  36.4 0.0 copy-start.2
  36.4 0.6 %copy-done.2 = f32[8,128]{1,0:T(8,128)} copy-done((f32[8,128]{1,0:T(8,128)}, f32[8,128]{1,0:T(8,128)S(1)}, u32[]{:S(2)}) %copy-start.2) | copy-done | bytes 4120
  37.0 1.8 %shard_map.51 = (f32[16,32,128]{2,1,0:T(8,128)}, f32[16,32,128]{2,1,0:T(8,128)}) custom-call(f32[16,32,128]{2,1,0:T(8,128)} %copy-done, f32[16,32,128]{2,1,0:T(8,128)} %copy-done.1, f32[8,128]{1,0:T(8,128)} %copy-done.2), custom_call_target="tpu_custom_call" | custom-call | tf_op jit(solution)/shard_map/pallas_call | solution.py:529
Async XLA Ops:
  35.1 0.7 %copy-start = (f32[16,32,128]{2,1,0:T(8,128)}, f32[16,32,128]{2,1,0:T(8,128)S(1)}, u32[]{:S(2)}) copy-start(f32[16,32,128]{2,1,0:T(8,128)S(1)} %get-tuple-element.5.psi_ref) | copy-start | bytes 786436
  35.8 0.7 %copy-start.1 = (f32[16,32,128]{2,1,0:T(8,128)}, f32[16,32,128]{2,1,0:T(8,128)S(1)}, u32[]{:S(2)}) copy-start(f32[16,32,128]{2,1,0:T(8,128)S(1)} %get-tuple-element.6.corr_ref) | copy-start | bytes 786436
  36.4 0.6 %copy-start.2 = (f32[8,128]{1,0:T(8,128)}, f32[8,128]{1,0:T(8,128)S(1)}, u32[]{:S(2)}) copy-start(f32[8,128]{1,0:T(8,128)S(1)} %get-tuple-element.7.scale_ref) | copy-start | bytes 12292

commit v2 on v1

v2 whole, which is shorter than its diff:
```python
import functools

import jax
import jax.numpy as jnp
from jax import lax
from jax.experimental import pallas as pl
from jax.experimental.pallas import tpu as pltpu
from jax.sharding import PartitionSpec as P

SUBSTEPS = 3
LAP_COEF = (-205.0 / 72.0, 8.0 / 5.0, -1.0 / 5.0, 8.0 / 315.0, -1.0 / 560.0)
STEP = 0.08
AXES = ("gx", "gy", "gz")
MESH = pl.DeviceIdType.MESH
R = 8
H = 4


def lanes(shape):
    return lax.broadcasted_iota(jnp.int32, shape, len(shape) - 1)


PARTNERS = [(dx, dy, dz) for dx in (-1, 0, 1) for dy in (-1, 0, 1) for dz in (-1, 0, 1) if dx or dy or dz]
GROUP = 4


def turn(value, shift):
    return value if isinstance(shift, int) and shift == 0 else pltpu.roll(value, shift, 1)


def modulo(a, n):
    return a % n if isinstance(a, int) else lax.rem(a, n)


def kernel(sizes, w_hbm, wave_hbm, ext_hbm, out_ref, corr_ref, scale_ref,
           wb, sb, yb, co, psi, va, part, pack, zin, zb, ypack, yin, bands, edges, rims, ext_ref, w_ref,
           sums, sums2, send, recv, send2, recv2, local):
    nx, ny, nz = sizes
    cx, cy, cz = wave_hbm.shape
    wave_ref = wb.at[pl.ds(R, cx), pl.ds(R, cy)]
    get_wave = pltpu.make_async_copy(wave_hbm, wave_ref, local.at[0])
    get_ext = pltpu.make_async_copy(ext_hbm, ext_ref, local.at[1])
    get_weights = pltpu.make_async_copy(w_hbm, w_ref, local.at[2])
    get_wave.start()
    get_weights.start()
    ix, iy, iz = (lax.axis_index(a) for a in AXES)
    plane = nx * nz
    per = cz // cx
    here = ix * nz + iz

    def plane_id(d):
        t = lax.rem(here + d, plane)
        return t, {"gx": lax.div(t, nz), "gz": lax.rem(t, nz)}

    def line_id(d):
        t = lax.rem(iy + d, ny)
        return t, {"gy": t}

    barrier = pltpu.get_barrier_semaphore()

    def greet(ids):
        def body(d, c):
            pl.semaphore_signal(barrier, inc=1, device_id=ids(d)[1], device_id_type=MESH)
            return c
        return body

    near = nx <= 4 and ny <= 4 and nz <= 2

    def greet_partners(partners):
        count = 0
        for d3 in partners:
            there = None
            target = {}
            for name, d, i, n in zip(AXES, d3, (ix, iy, iz), sizes):
                if d:
                    ok = i < n - 1 if d > 0 else i > 0
                    there = ok if there is None else there & ok
                    target[name] = jnp.clip(i + d, 0, n - 1)
            count += there.astype(jnp.int32)

            @pl.when(there)
            def _(target=target):
                pl.semaphore_signal(barrier, inc=1, device_id=target, device_id_type=MESH)
        return count

    if near:
        guests = greet_partners(PARTNERS)
    else:
        guests = plane - 1 + ny - 1 + greet_partners([d for d in PARTNERS if d[1] and (d[0] or d[2])])
        lax.fori_loop(1, plane, greet(plane_id), 0)
        lax.fori_loop(1, ny, greet(line_id), 0)

    counter = [0]

    def message(src, dst, dx, dy, dz):
        k = counter[0]
        counter[0] += 1
        to, back = None, None
        for d, i, n in ((dx, ix, nx), (dy, iy, ny), (dz, iz, nz)):
            if d > 0:
                a, b = i < n - 1, i > 0
            elif d < 0:
                a, b = i > 0, i < n - 1
            else:
                continue
            to = a if to is None else to & a
            back = b if back is None else back & b
        target = {}
        for name, d, i, n in zip(AXES, (dx, dy, dz), (ix, iy, iz), sizes):
            if d:
                target[name] = jnp.clip(i + d, 0, n - 1)
        copy = pltpu.make_async_remote_copy(
            src_ref=src, dst_ref=dst, send_sem=send.at[k], recv_sem=recv.at[k],
            device_id=target, device_id_type=MESH)
        return copy, to, back, dst

    sent = []

    def start(messages):
        for copy, to, _, _ in messages:
            pl.when(to)(copy.start)
            sent.append((copy, to))

    def blank(messages):
        for _, _, back, dst in messages:
            @pl.when(jnp.logical_not(back))
            def _(dst=dst):
                dst[...] = jnp.zeros(dst.shape, dst.dtype)

    def arrive(messages):
        for copy, _, back, _ in messages:
            pl.when(back)(copy.wait_recv)

    at = lanes((cy, cz))
    zero = jnp.zeros((cy, cz), jnp.float32)

    def pack_one(i, value, packs):
        mine = (at >= per * i) & (at < per * i + per)
        low = turn(value, per * i)
        high = turn(value, modulo(per * i + per, cz))
        return jnp.where(mine, low, packs[0]), jnp.where(mine, high, packs[1])

    def pack_out(slot, packs):
        pack[slot, 0] = packs[0]
        pack[slot, 1] = packs[1]

    def z_messages(slot, dxs, dys):
        out = []
        for dx in dxs:
            for dy in dys:
                if dy > 0:
                    rows, into = pl.ds(cy - R, R), pl.ds(0, R)
                elif dy < 0:
                    rows, into = pl.ds(0, R), pl.ds(R + cy, R)
                else:
                    rows, into = pl.ds(0, cy), pl.ds(R, cy)
                out.append(message(pack.at[slot, 1, rows], zin.at[slot, 0, 1 - dx, into], dx, dy, 1))
                out.append(message(pack.at[slot, 0, rows], zin.at[slot, 1, 1 - dx, into], dx, dy, -1))
        return out

    def side_messages(src, dst, moves):
        out = []
        for dx, dy in moves:
            if dx > 0:
                sx, tx = pl.ds(cx - R, R), pl.ds(0, R)
            elif dx < 0:
                sx, tx = pl.ds(0, R), pl.ds(R + cx, R)
            else:
                sx, tx = pl.ds(0, cx), pl.ds(R, cx)
            if dy > 0:
                sy, ty = pl.ds(cy - R, R), pl.ds(0, R)
            elif dy < 0:
                sy, ty = pl.ds(0, R), pl.ds(R + cy, R)
            else:
                sy, ty = pl.ds(0, cy), pl.ds(R, cy)
            out.append(message(src.at[sx, sy], dst.at[tx, ty], dx, dy, 0))
        return out

    face_x = [(dx, 0) for dx in (1, -1)]
    face_y = [(0, dy) for dy in (1, -1)]
    edge_xy = [(dx, dy) for dx in (1, -1) for dy in (1, -1)]
    src_ref = sb.at[pl.ds(R, cx), pl.ds(R, cy)]
    wave_x, wave_y, wave_xy = (side_messages(wave_hbm, wb, m) for m in (face_x, face_y, edge_xy))
    wave_z, wave_e = z_messages(0, (-1, 0, 1), (0,)), z_messages(0, (-1, 0, 1), (-1, 1))
    src_x, src_y, src_xy = (side_messages(src_ref, sb, m) for m in (face_x, face_y, edge_xy))
    src_z, src_e = z_messages(1, (-1, 0, 1), (0,)), z_messages(1, (-1, 0, 1), (-1, 1))

    psi_moves = []
    for s in range(SUBSTEPS - 1):
        buf = psi.at[s]
        moves = [
            message(buf.at[pl.ds(cx, H), pl.ds(R, cy)], buf.at[pl.ds(0, H), pl.ds(R, cy)], 1, 0, 0),
            message(buf.at[pl.ds(H, H), pl.ds(R, cy)], buf.at[pl.ds(H + cx, H), pl.ds(R, cy)], -1, 0, 0),
        ]
        moves += [
            message(ypack.at[s, 1], yin.at[s, 0], 0, 1, 0),
            message(ypack.at[s, 0], yin.at[s, 1], 0, -1, 0),
        ]
        moves += z_messages(2 + s, (0,), (0,))
        psi_moves.append(moves)

    get_wave.wait()
    packs = (zero, zero)
    for i in range(cx):
        packs = pack_one(i, wave_ref[i], packs)
    pack_out(0, packs)
    pl.semaphore_wait(barrier, guests)
    start(wave_e + wave_x + wave_z + wave_y + wave_xy)
    get_ext.start()
    for group in [wave_x, wave_y, wave_xy, wave_z, wave_e, src_x, src_y, src_xy, src_z, src_e] + psi_moves:
        blank(group)
    get_weights.wait()

    def taps_of(dim, flip):
        return [(k, w_ref[dim, R - k if flip else R + k]) for k in range(-R, R + 1)]

    row = lax.broadcasted_iota(jnp.int32, (cz, cz), 0)
    gap = row - lanes((cz, cz))
    gains = [STEP * 0.5 * c for c in LAP_COEF]
    z_taps = [taps_of(2, False), taps_of(2, True), [(k, gains[abs(k)]) for k in range(-H, H + 1) if k]]

    def dot(a, b):
        return jnp.dot(a, b, precision=lax.Precision.HIGHEST, preferred_element_type=jnp.float32)

    for slot, taps in enumerate(z_taps):
        inner = jnp.zeros((cz, cz), jnp.float32)
        for k, tap in taps:
            inner = jnp.where(gap == k, tap, inner)
        bands[slot] = inner

    tile = (per, cz)
    lane = lanes(tile)
    cell = lax.rem(lane, per)
    apart = lax.broadcasted_iota(jnp.int32, tile, 0) - cell
    group_of = lax.div(lane, per)
    owner = [group_of, lax.rem(group_of + 1, cx)]
    none = jnp.zeros(tile, jnp.float32)

    def corner(side, taps):
        shift = per if side == 0 else -per
        made = none
        for k, tap in taps:
            made = jnp.where(apart == k + shift, tap, made)
        return made

    for flip in range(2):
        taps = dict(taps_of(0, bool(flip)))
        for side in range(2):
            by_z = corner(side, [(k, tap) for k, tap in z_taps[flip] if (k < 0) == (side == 0) and k])
            is_owner = [owner[side] == q for q in range(cx)]
            for t in range(2 * cx):
                at_plane = t if t < cx else (t if t - cx < cx // 2 else t - 2 * cx)
                by_x = none
                for q in range(cx):
                    if at_plane - q in taps:
                        by_x = jnp.where(is_owner[q], taps[at_plane - q], by_x)
                edges[flip, side, pl.ds(per * t, per)] = by_x * by_z
    for side in range(2):
        by_z = corner(side, [(k, tap) for k, tap in z_taps[2] if (k < 0) == (side == 0)])
        for t in range(cx):
            rims[side, pl.ds(per * t, per)] = jnp.where(owner[side] == t, by_z, none)

    even = lax.rem(lax.div(at, per), 2) == 0

    def rim_pair(sides):
        return jnp.where(even, sides[0], sides[1]), jnp.where(even, sides[1], sides[0])

    def from_rim(pair, i, width):
        return jnp.where((at < width) | (at >= cz - width), turn(pair[i % 2], modulo(cz - per * i, cz)), zero)

    def planes(buf, first, count, rows):
        return buf[pl.ds(first, count), rows].reshape(count * rows.size, cz)

    def smear(src, slot, square, flip, faces, packs_in, late):
        taps_x, taps_y = taps_of(0, flip), taps_of(1, flip)

        def along_x(first):
            ins = [src[k, pl.ds(R + first, 8)] for k in range(cx + 2 * R)]
            if square:
                ins = [v * v for v in ins]
            for i in range(cx):
                total = None
                for k, tap in taps_x:
                    part_ = ins[i + R + k] * tap
                    total = part_ if total is None else total + part_
                yb[i, pl.ds(R + first, 8)] = total

        arrive(faces)
        for first in range(0, cy, 8):
            along_x(first)
        own = pl.ds(R, cy)
        for g in range(0, cx, cx // 2):
            yb[pl.ds(g, cx // 2), own] = dot(planes(yb, g, cx // 2, own), bands[int(flip)]).reshape(cx // 2, cy, cz)
        arrive(packs_in)
        wide = lanes((cy + 2 * R, cz)) < cz // 2
        for side in range(2):
            mine = zin[slot, side, 1]
            other = jnp.where(wide, zin[slot, side, 2], zin[slot, side, 0])
            if square:
                mine, other = mine * mine, other * other
            zb[side] = dot(jnp.concatenate([mine, other], 1), edges[int(flip), side])
        pair = []
        for side in range(2):
            total = zero
            for k, tap in taps_y:
                total = total + zb[side, pl.ds(R + k, cy)] * tap
            pair.append(total)
        pair = rim_pair(pair)
        for i in range(cx):
            total = from_rim(pair, i, R)
            low, mid, high = total[:8], total[8:cy - 8], total[cy - 8:]
            for k, tap in taps_y:
                if k >= 0:
                    low = low + yb[i, pl.ds(R + k, 8)] * tap
                mid = mid + yb[i, pl.ds(R + 8 + k, cy - 16)] * tap
                if k <= 0:
                    high = high + yb[i, pl.ds(R + cy - 8 + k, 8)] * tap
            co[i] = jnp.concatenate([low, mid, high], 0)
        arrive(late)
        for first in (-8, cy):
            along_x(first)
            rows = pl.ds(R + first, 8)
            yb[:, rows] = dot(planes(yb, 0, cx, rows), bands[int(flip)]).reshape(cx, 8, cz)

        def result(i):
            low, high = co[i, pl.ds(0, 8)], co[i, pl.ds(cy - 8, 8)]
            for k, tap in taps_y:
                if k < 0:
                    low = low + yb[i, pl.ds(R + k, 8)] * tap
                if k > 0:
                    high = high + yb[i, pl.ds(R + cy - 8 + k, 8)] * tap
            return jnp.concatenate([low, co[i, pl.ds(8, cy - 16)], high], 0)

        return result

    smeared = smear(wb, 0, True, False, wave_x, wave_z + wave_e, wave_y + wave_xy)
    packs = (zero, zero)
    for i in range(cx):
        coarse = smeared(i)
        value = wave_ref[i]
        dens = value * value
        both = coarse * coarse
        source = 0.5 * dens * both - dens * coarse
        corr_ref[i] = (0.5 / 3.0) * both * coarse - 0.5 * both
        sb[R + i, pl.ds(R, cy)] = source
        packs = pack_one(i, source, packs)
    pack_out(1, packs)
    start(src_e + src_x + src_z + src_y + src_xy)

    def z_rim(slot):
        return rim_pair([dot(zin[slot, side, 1, pl.ds(R, cy)], rims[side]) for side in range(2)])

    def own_part(buf, reach, weight, first_step):
        pair = z_rim(0) if first_step else None
        own = pl.ds(R, cy)
        for g in range(0, cx, GROUP):
            along = dot(planes(buf, reach + g, GROUP, own), bands[2])
            for i in range(g, g + GROUP):
                total = buf[reach + i, own] * weight(i) + along[(i - g) * cy:(i - g + 1) * cy]
                if first_step:
                    total = total + from_rim(pair, i, H)
                for k in range(1, H + 1):
                    pairs = [buf[reach + j, own] for j in (i - k, i + k) if first_step or 0 <= j < cx]
                    if first_step:
                        pairs += [buf[reach + i, pl.ds(R + j, cy)] for j in (-k, k)]
                    both = pairs[0]
                    for p in pairs[1:]:
                        both = both + p
                    total = total + gains[k] * both
                if not first_step:
                    up = down = None
                    for k in range(1, H + 1):
                        a = gains[k] * buf[reach + i, pl.ds(R + k, cy - 8)]
                        b = gains[k] * buf[reach + i, pl.ds(R + 8 - k, cy - 8)]
                        up, down = (a, b) if up is None else (up + a, down + b)
                    total = total + jnp.concatenate([up[:8], up[8:] + down[:cy - 16], down[cy - 16:]], 0)
                part[i] = total

    def halo_part(buf, pair, i):
        total = part[i] + from_rim(pair, i, H)
        for k in range(1, H + 1):
            for j in (i - k, i + k):
                if not 0 <= j < cx:
                    total = total + gains[k] * buf[H + j, pl.ds(R, cy)]
        low, high = total[:8], total[cy - 8:]
        for k in range(1, H + 1):
            low = low + gains[k] * buf[H + i, pl.ds(R - k, 8)]
            high = high + gains[k] * buf[H + i, pl.ds(R + cy - 8 + k, 8)]
        return jnp.concatenate([low, total[8:cy - 8], high], 0)

    middle = 1.0 + STEP * 0.5 * 3.0 * LAP_COEF[0]
    own_part(wb, R, lambda i: middle, True)
    smeared = smear(sb, 1, False, True, src_x, src_z + src_e, src_y + src_xy)
    get_ext.wait()
    groups = [list(range(g, g + GROUP)) for g in range(0, cx, GROUP)]
    groups = groups[:1] + groups[-1:] + groups[1:-1]

    def first_step(i):
        corr = corr_ref[i] + smeared(i)
        corr_ref[i] = corr
        felt = STEP * (corr + ext_ref[i])
        va[i] = middle - felt
        return part[i] - felt * wave_ref[i]

    def send_out(s, step):
        after = psi.at[s]
        packs = (zero, zero)
        for n_, these in enumerate(groups):
            for i in these:
                value = step(i)
                after[H + i, pl.ds(R, cy)] = value
                packs = pack_one(i, value, packs)
                half = pl.ds(H * (i % 2), H)
                ypack[s, 0, i // 2, half] = value[:H]
                ypack[s, 1, i // 2, half] = value[cy - H:]
            if n_ == 1:
                start(psi_moves[s][:2])
        pack_out(2 + s, packs)
        start(psi_moves[s][2:])

    send_out(0, first_step)
    total = zero
    for s in range(SUBSTEPS - 1):
        buf = psi.at[s]
        own_part(buf, H, lambda i: va[i], False)
        arrive(psi_moves[s])
        for i in range(cx):
            half = pl.ds(H * (i % 2), H)
            buf[H + i, pl.ds(R - H, H)] = yin[s, 0, i // 2, half]
            buf[H + i, pl.ds(R + cy, H)] = yin[s, 1, i // 2, half]
        pair = z_rim(2 + s)
        if s < SUBSTEPS - 2:
            send_out(s + 1, lambda i: halo_part(buf, pair, i))
        else:
            for i in range(cx):
                value = halo_part(buf, pair, i)
                out_ref[i] = value
                total = total + value * value

    partial = jnp.sum(total, axis=0, keepdims=True)
    everyone = plane * ny
    me = iy * plane + here

    def any_id(d):
        t = lax.rem(me + d, everyone)
        p = lax.rem(t, plane)
        return t, {"gx": lax.div(p, nz), "gy": lax.div(t, plane), "gz": lax.rem(p, nz)}

    def all_sum(value, slots, ssem, rsem, me, n, ids):
        if n == 1:
            return value
        slots[me] = value

        def copy_of(d, slot):
            return pltpu.make_async_remote_copy(
                src_ref=slots.at[me], dst_ref=slots.at[slot], send_sem=ssem.at[d], recv_sem=rsem.at[slot],
                device_id=ids(d)[1], device_id_type=MESH)

        def go(d, c):
            copy_of(d, me).start()
            return c

        def come(d, c):
            copy_of(d, ids(d)[0]).wait_recv()
            return c

        def left(d, c):
            copy_of(d, me).wait_send()
            return c

        lax.fori_loop(1, n, go, 0)
        lax.fori_loop(1, n, come, 0)
        total = jnp.sum(slots[...], axis=0)
        lax.fori_loop(1, n, left, 0)
        return total

    if near:
        sums[0] = partial
        for d in range(1, everyone):
            pltpu.make_async_remote_copy(
                src_ref=sums.at[0], dst_ref=sums.at[d], send_sem=send2.at[0, 0], recv_sem=recv2.at[0, 0],
                device_id=any_id(d)[1], device_id_type=MESH).start()
        rest = sums.at[pl.ds(1, everyone - 1)]
        whole = pltpu.make_async_remote_copy(
            src_ref=rest, dst_ref=rest, send_sem=send2.at[0, 0], recv_sem=recv2.at[0, 0],
            device_id=any_id(1)[1], device_id_type=MESH)
        whole.wait_recv()
        partial = jnp.sum(sums[...], axis=0)
    else:
        partial = all_sum(partial, sums, send2.at[0], recv2.at[0], here, plane, plane_id)
        partial = all_sum(partial, sums2, send2.at[1], recv2.at[1], iy, ny, line_id)
    cells = float(cx * cy * cz * nx * ny * nz)
    scale_ref[...] = lax.rsqrt(jnp.full(scale_ref.shape, jnp.sum(partial), jnp.float32) / cells + 1e-06)
    for copy, to in sent:
        pl.when(to)(copy.wait_send)
    if near:
        whole.wait_send()


def finish(psi_ref, corr_ref, scale_ref, out_hbm, corr_hbm, scaled, sems):
    copies = [pltpu.make_async_copy(corr_ref, corr_hbm, sems.at[0])]
    copies[0].start()
    cx, cy, cz = psi_ref.shape
    scale = scale_ref[0:1]
    steps = 2 if cx % 2 == 0 else 1
    for n in range(steps):
        some = pl.ds(n * (cx // steps), cx // steps)
        scaled[some] = psi_ref[some] * scale.reshape(1, 1, cz)
        copies.append(pltpu.make_async_copy(scaled.at[some], out_hbm.at[some], sems.at[1 + n]))
        copies[-1].start()
    for copy in copies:
        copy.wait()


def shards(sizes, wave, external, weights):
    cx, cy, cz = wave.shape
    nx, ny, nz = sizes
    f32 = jnp.float32
    n_messages = 72
    summed = nx * ny * nz if nx <= 4 and ny <= 4 and nz <= 2 else nx * nz
    most = max(summed, ny)
    vmem = pl.BlockSpec(memory_space=pltpu.VMEM)
    stay = pl.BlockSpec(memory_space=pltpu.HBM)
    psi, corr, scale = pl.pallas_call(
        functools.partial(kernel, sizes),
        out_shape=(jax.ShapeDtypeStruct(wave.shape, f32), jax.ShapeDtypeStruct(wave.shape, f32),
                   jax.ShapeDtypeStruct((8, cz), f32)),
        in_specs=[stay, stay, stay],
        out_specs=(vmem, vmem, vmem),
        scratch_shapes=[
            pltpu.VMEM((cx + 2 * R, cy + 2 * R, cz), f32),
            pltpu.VMEM((cx + 2 * R, cy + 2 * R, cz), f32),
            pltpu.VMEM((cx, cy + 2 * R, cz), f32),
            pltpu.VMEM((cx, cy, cz), f32),
            pltpu.VMEM((SUBSTEPS - 1, cx + 2 * H, cy + 2 * R, cz), f32),
            pltpu.VMEM((cx, cy, cz), f32),
            pltpu.VMEM((cx, cy, cz), f32),
            pltpu.VMEM((SUBSTEPS + 1, 2, cy, cz), f32),
            pltpu.VMEM((SUBSTEPS + 1, 2, 3, cy + 2 * R, cz), f32),
            pltpu.VMEM((2, cy + 2 * R, cz), f32),
            pltpu.VMEM((SUBSTEPS - 1, 2, cx // 2, 2 * H, cz), f32),
            pltpu.VMEM((SUBSTEPS - 1, 2, cx // 2, 2 * H, cz), f32),
            pltpu.VMEM((3, cz, cz), f32),
            pltpu.VMEM((2, 2, 2 * cz, cz), f32),
            pltpu.VMEM((2, cz, cz), f32),
            pltpu.VMEM((cx, cy, cz), f32),
            pltpu.SMEM(weights.shape, f32),
            pltpu.VMEM((summed, 1, cz), f32),
            pltpu.VMEM((ny, 1, cz), f32),
            pltpu.SemaphoreType.DMA((n_messages,)),
            pltpu.SemaphoreType.DMA((n_messages,)),
            pltpu.SemaphoreType.DMA((2, most)),
            pltpu.SemaphoreType.DMA((2, most)),
            pltpu.SemaphoreType.DMA((3,)),
        ],
        compiler_params=pltpu.CompilerParams(collective_id=0, has_side_effects=True,
                                             vmem_limit_bytes=48 * 1024 * 1024),
    )(*[pltpu.with_memory_space_constraint(x, pltpu.HBM) for x in (weights, wave, external)])
    return pl.pallas_call(
        finish,
        out_shape=(jax.ShapeDtypeStruct(wave.shape, f32), jax.ShapeDtypeStruct(wave.shape, f32)),
        in_specs=[vmem, vmem, vmem],
        out_specs=(stay, stay),
        scratch_shapes=[pltpu.VMEM((cx, cy, cz), f32), pltpu.SemaphoreType.DMA((3,))],
    )(*[pltpu.with_memory_space_constraint(x, pltpu.VMEM) for x in (psi, corr, scale)])


def solution(mesh):
    sizes = tuple(mesh.shape[a] for a in AXES)
    spec = P(*AXES)
    return jax.shard_map(
        functools.partial(shards, sizes),
        mesh=mesh,
        in_specs=(spec, spec, P()),
        out_specs=(spec, spec),
        check_vma=False,
    )
```

time: 39 us -> 34 us (0.87)
  Pallas kernels: 36.3 us -> 33.2 us
  local copies, waits for them, and re-layouts: 1.97 us -> 0 us
    pallas_call x1, Pallas kernels: 34.4 us -> 32.4 us  [shards(): pl.pallas_call(functools.partial(kernel, sizes), out_shape=(jax.ShapeDtyp...]
    unnamed x6 -> x0, local copies, waits for them, and re-layouts: 1.97 us -> none
    pallas_call x1, Pallas kernels: 1.84 us -> 0.81 us  [shards(): pl.pallas_call(finish, out_shape=(jax.ShapeDtypeStruct(wave.shape, f32),...]
where the time goes in v2:
time: 34 us; the launch traced here: 33.8 us
  Pallas kernels  33.2 us (98%)
  between operations  0.64 us (2%)
    pallas_call x1, Pallas kernels, shards(): pl.pallas_call(functools.partial(kernel, sizes), out_shape=(jax.ShapeDtyp...  32.4 us
    pallas_call x1, Pallas kernels, shards(): pl.pallas_call(finish, out_shape=(jax.ShapeDtypeStruct(wave.shape, f32),...  0.81 us

profile of v2, /device:TPU:0, one launch (start us, length us, event | category | flops | bytes accessed | tf_op | source)
XLA Modules:
  0.0 33.8 jit_solution(10547228722279091889)
XLA Ops:
  0.6 32.4 %shard_map.50 = (f32[16,32,128]{2,1,0:T(8,128)S(1)}, f32[16,32,128]{2,1,0:T(8,128)S(1)}, f32[8,128]{1,0:T(8,128)S(1)}) custom-call(f32[3,17]{1,0:T(4,128)} %w_hbm.1, f32[16,32,128]{2,1,0:T(8,128)} %wave_hbm.1, f32[16,32,128]{2,1,0:T(8,128)} %ext_hbm.1), custom_call_target="tpu_custom_call" | custom-call | tf_op jit(solution)/shard_map/pallas_call | solution.py:524
  33.0 0.8 %shard_map.51 = (f32[16,32,128]{2,1,0:T(8,128)}, f32[16,32,128]{2,1,0:T(8,128)}) custom-call(f32[16,32,128]{2,1,0:T(8,128)S(1)} %get-tuple-element.5.psi_ref, f32[16,32,128]{2,1,0:T(8,128)S(1)} %get-tuple-element.6.corr_ref, f32[8,128]{1,0:T(8,128)S(1)} %get-tuple-element.7.scale_ref), custom_call_target="tpu_custom_call" | custom-call | tf_op jit(solution)/shard_map/pallas_call | solution.py:559

commit v3 on v2

--- a/solution.py
+++ b/solution.py
@@ -33,7 +33,7 @@
 
 
 def kernel(sizes, w_hbm, wave_hbm, ext_hbm, out_ref, corr_ref, scale_ref,
-           wb, sb, yb, co, psi, va, part, pack, zin, zb, ypack, yin, bands, edges, rims, ext_ref, w_ref,
+           wb, sb, yb, co, psi, va, part, pack, zin, zb, ypack, yin, bands, edges, rims, blanks, spare, ext_ref, w_ref,
            sums, sums2, send, recv, send2, recv2, local):
     nx, ny, nz = sizes
     cx, cy, cz = wave_hbm.shape
@@ -90,11 +90,16 @@
         lax.fori_loop(1, plane, greet(plane_id), 0)
         lax.fori_loop(1, ny, greet(line_id), 0)
 
-    counter = [0]
-
-    def message(src, dst, dx, dy, dz):
-        k = counter[0]
-        counter[0] += 1
+    blanks[...] = jnp.zeros(blanks.shape, jnp.float32)
+    sent_rows = {}
+
+    def rows_of(ref):
+        count = 1
+        for n in ref.shape[:-1]:
+            count *= n
+        return count
+
+    def message(src, dst, dx, dy, dz, group):
         to, back = None, None
         for d, i, n in ((dx, ix, nx), (dy, iy, ny), (dz, iz, nz)):
             if d > 0:
@@ -109,27 +114,33 @@
         for name, d, i, n in zip(AXES, (dx, dy, dz), (ix, iy, iz), sizes):
             if d:
                 target[name] = jnp.clip(i + d, 0, n - 1)
+        way = PARTNERS.index((dx, dy, dz))
+        rows, _ = sent_rows.get(way, (0, to))
+        sent_rows[way] = rows + rows_of(dst), to
         copy = pltpu.make_async_remote_copy(
-            src_ref=src, dst_ref=dst, send_sem=send.at[k], recv_sem=recv.at[k],
+            src_ref=src, dst_ref=dst, send_sem=send.at[way], recv_sem=recv.at[group],
             device_id=target, device_id_type=MESH)
-        return copy, to, back, dst
-
-    sent = []
+        return copy, to, back, dst, group
 
     def start(messages):
-        for copy, to, _, _ in messages:
+        for copy, to, *_ in messages:
             pl.when(to)(copy.start)
-            sent.append((copy, to))
 
     def blank(messages):
-        for _, _, back, dst in messages:
-            @pl.when(jnp.logical_not(back))
-            def _(dst=dst):
-                dst[...] = jnp.zeros(dst.shape, dst.dtype)
+        for _, _, back, dst, group in messages:
+            first = [pl.ds(0, n) for n in dst.shape[:-1]]
+            src = blanks.at[tuple(first) if len(first) == 2 else (0, *first)]
+            pl.when(jnp.logical_not(back))(pltpu.make_async_copy(src, dst, recv.at[group]).start)
+
+    def bytes_of(rows, send_sem, recv_sem):
+        some = spare.at[pl.ds(0, rows)]
+        return pltpu.make_async_remote_copy(
+            src_ref=some, dst_ref=some, send_sem=send_sem, recv_sem=recv_sem,
+            device_id={"gx": ix}, device_id_type=MESH)
 
     def arrive(messages):
-        for copy, _, back, _ in messages:
-            pl.when(back)(copy.wait_recv)
+        group = messages[0][-1]
+        bytes_of(sum(rows_of(m[3]) for m in messages), send.at[0], recv.at[group]).wait_recv()
 
     at = lanes((cy, cz))
     zero = jnp.zeros((cy, cz), jnp.float32)
@@ -144,7 +155,7 @@
         pack[slot, 0] = packs[0]
         pack[slot, 1] = packs[1]
 
-    def z_messages(slot, dxs, dys):
+    def z_messages(slot, dxs, dys, group):
         out = []
         for dx in dxs:
             for dy in dys:
@@ -154,11 +165,11 @@
                     rows, into = pl.ds(0, R), pl.ds(R + cy, R)
                 else:
                     rows, into = pl.ds(0, cy), pl.ds(R, cy)
-                out.append(message(pack.at[slot, 1, rows], zin.at[slot, 0, 1 - dx, into], dx, dy, 1))
-                out.append(message(pack.at[slot, 0, rows], zin.at[slot, 1, 1 - dx, into], dx, dy, -1))
+                out.append(message(pack.at[slot, 1, rows], zin.at[slot, 0, 1 - dx, into], dx, dy, 1, group))
+                out.append(message(pack.at[slot, 0, rows], zin.at[slot, 1, 1 - dx, into], dx, dy, -1, group))
         return out
 
-    def side_messages(src, dst, moves):
+    def side_messages(src, dst, moves, group):
         out = []
         for dx, dy in moves:
             if dx > 0:
@@ -173,39 +184,41 @@
                 sy, ty = pl.ds(0, R), pl.ds(R + cy, R)
             else:
                 sy, ty = pl.ds(0, cy), pl.ds(R, cy)
-            out.append(message(src.at[sx, sy], dst.at[tx, ty], dx, dy, 0))
+            out.append(message(src.at[sx, sy], dst.at[tx, ty], dx, dy, 0, group))
         return out
 
     face_x = [(dx, 0) for dx in (1, -1)]
     face_y = [(0, dy) for dy in (1, -1)]
     edge_xy = [(dx, dy) for dx in (1, -1) for dy in (1, -1)]
     src_ref = sb.at[pl.ds(R, cx), pl.ds(R, cy)]
-    wave_x, wave_y, wave_xy = (side_messages(wave_hbm, wb, m) for m in (face_x, face_y, edge_xy))
-    wave_z, wave_e = z_messages(0, (-1, 0, 1), (0,)), z_messages(0, (-1, 0, 1), (-1, 1))
-    src_x, src_y, src_xy = (side_messages(src_ref, sb, m) for m in (face_x, face_y, edge_xy))
-    src_z, src_e = z_messages(1, (-1, 0, 1), (0,)), z_messages(1, (-1, 0, 1), (-1, 1))
+    wave_x, src_x = side_messages(wave_hbm, wb, face_x, 0), side_messages(src_ref, sb, face_x, 3)
+    wave_y, src_y = side_messages(wave_hbm, wb, face_y, 2), side_messages(src_ref, sb, face_y, 5)
+    wave_xy, src_xy = side_messages(wave_hbm, wb, edge_xy, 2), side_messages(src_ref, sb, edge_xy, 5)
+    wave_z, src_z = z_messages(0, (-1, 0, 1), (0,), 1), z_messages(1, (-1, 0, 1), (0,), 4)
+    wave_e, src_e = z_messages(0, (-1, 0, 1), (-1, 1), 1), z_messages(1, (-1, 0, 1), (-1, 1), 4)
 
     psi_moves = []
     for s in range(SUBSTEPS - 1):
         buf = psi.at[s]
         moves = [
-            message(buf.at[pl.ds(cx, H), pl.ds(R, cy)], buf.at[pl.ds(0, H), pl.ds(R, cy)], 1, 0, 0),
-            message(buf.at[pl.ds(H, H), pl.ds(R, cy)], buf.at[pl.ds(H + cx, H), pl.ds(R, cy)], -1, 0, 0),
+            message(buf.at[pl.ds(cx, H), pl.ds(R, cy)], buf.at[pl.ds(0, H), pl.ds(R, cy)], 1, 0, 0, 6 + s),
+            message(buf.at[pl.ds(H, H), pl.ds(R, cy)], buf.at[pl.ds(H + cx, H), pl.ds(R, cy)], -1, 0, 0, 6 + s),
         ]
         moves += [
-            message(ypack.at[s, 1], yin.at[s, 0], 0, 1, 0),
-            message(ypack.at[s, 0], yin.at[s, 1], 0, -1, 0),
+            message(ypack.at[s, 1], yin.at[s, 0], 0, 1, 0, 6 + s),
+            message(ypack.at[s, 0], yin.at[s, 1], 0, -1, 0, 6 + s),
         ]
-        moves += z_messages(2 + s, (0,), (0,))
+        moves += z_messages(2 + s, (0,), (0,), 6 + s)
         psi_moves.append(moves)
 
+    pl.semaphore_wait(barrier, guests)
+    start(wave_x + wave_y + wave_xy)
     get_wave.wait()
     packs = (zero, zero)
     for i in range(cx):
         packs = pack_one(i, wave_ref[i], packs)
     pack_out(0, packs)
-    pl.semaphore_wait(barrier, guests)
-    start(wave_e + wave_x + wave_z + wave_y + wave_xy)
+    start(wave_e + wave_z)
     get_ext.start()
     for group in [wave_x, wave_y, wave_xy, wave_z, wave_e, src_x, src_y, src_xy, src_z, src_e] + psi_moves:
         blank(group)
@@ -219,14 +232,27 @@
     gains = [STEP * 0.5 * c for c in LAP_COEF]
     z_taps = [taps_of(2, False), taps_of(2, True), [(k, gains[abs(k)]) for k in range(-H, H + 1) if k]]
 
+    def halves(a):
+        high = a.astype(jnp.bfloat16)
+        return high, (a - high.astype(jnp.float32)).astype(jnp.bfloat16)
+
+    def keep(ref, index, a):
+        high, low = halves(a)
+        k = a.shape[0]
+        ref[(*index, pl.ds(0, k), pl.ds(0, cz))] = high
+        ref[(*index, pl.ds(0, k), pl.ds(cz, cz))] = low
+        ref[(*index, pl.ds(k, k), pl.ds(0, cz))] = high
+        ref[(*index, pl.ds(k, k), pl.ds(cz, cz))] = jnp.zeros_like(low)
+
     def dot(a, b):
-        return jnp.dot(a, b, precision=lax.Precision.HIGHEST, preferred_element_type=jnp.float32)
+        both = jnp.dot(jnp.concatenate(halves(a), 1), b, preferred_element_type=jnp.float32)
+        return both[:, :cz] + both[:, cz:]
 
     for slot, taps in enumerate(z_taps):
         inner = jnp.zeros((cz, cz), jnp.float32)
         for k, tap in taps:
             inner = jnp.where(gap == k, tap, inner)
-        bands[slot] = inner
+        keep(bands, (slot,), inner)
 
     tile = (per, cz)
     lane = lanes(tile)
@@ -248,17 +274,18 @@
         for side in range(2):
             by_z = corner(side, [(k, tap) for k, tap in z_taps[flip] if (k < 0) == (side == 0) and k])
             is_owner = [owner[side] == q for q in range(cx)]
+            rows = []
             for t in range(2 * cx):
                 at_plane = t if t < cx else (t if t - cx < cx // 2 else t - 2 * cx)
                 by_x = none
                 for q in range(cx):
                     if at_plane - q in taps:
                         by_x = jnp.where(is_owner[q], taps[at_plane - q], by_x)
-                edges[flip, side, pl.ds(per * t, per)] = by_x * by_z
+                rows.append(by_x * by_z)
+            keep(edges, (flip, side), jnp.concatenate(rows, 0))
     for side in range(2):
         by_z = corner(side, [(k, tap) for k, tap in z_taps[2] if (k < 0) == (side == 0)])
-        for t in range(cx):
-            rims[side, pl.ds(per * t, per)] = jnp.where(owner[side] == t, by_z, none)
+        keep(rims, (side,), jnp.concatenate([jnp.where(owner[side] == t, by_z, none) for t in range(cx)], 0))
 
     even = lax.rem(lax.div(at, per), 2) == 0
 
@@ -274,23 +301,41 @@
     def smear(src, slot, square, flip, faces, packs_in, late):
         taps_x, taps_y = taps_of(0, flip), taps_of(1, flip)
 
-        def along_x(first):
-            ins = [src[k, pl.ds(R + first, 8)] for k in range(cx + 2 * R)]
-            if square:
-                ins = [v * v for v in ins]
+        def load(k, first):
+            v = src[k, pl.ds(R + first, 8)]
+            return v * v if square else v
+
+        def along_x(first, own, other, init):
+            ins = {k: load(k, first) for k in range(cx + 2 * R) if (own if R <= k < R + cx else other)}
             for i in range(cx):
-                total = None
+                total = yb[i, pl.ds(R + first, 8)] if init else None
                 for k, tap in taps_x:
-                    part_ = ins[i + R + k] * tap
-                    total = part_ if total is None else total + part_
-                yb[i, pl.ds(R + first, 8)] = total
-
+                    if i + R + k in ins:
+                        part_ = ins[i + R + k] * tap
+                        total = part_ if total is None else total + part_
+                if total is not None:
+                    yb[i, pl.ds(R + first, 8)] = total
+
+        for first in range(0, cy, 8):
+            along_x(first, True, False, False)
         arrive(faces)
         for first in range(0, cy, 8):
-            along_x(first)
+            along_x(first, False, True, True)
         own = pl.ds(R, cy)
         for g in range(0, cx, cx // 2):
             yb[pl.ds(g, cx // 2), own] = dot(planes(yb, g, cx // 2, own), bands[int(flip)]).reshape(cx // 2, cy, cz)
+        for i in range(cx):
+            low = mid = high = None
+            for k, tap in taps_y:
+                a = yb[i, pl.ds(R + 8 + k, cy - 16)] * tap
+                mid = a if mid is None else mid + a
+                if k >= 0:
+                    a = yb[i, pl.ds(R + k, 8)] * tap
+                    low = a if low is None else low + a
+                if k <= 0:
+                    a = yb[i, pl.ds(R + cy - 8 + k, 8)] * tap
+                    high = a if high is None else high + a
+            co[i] = jnp.concatenate([low, mid, high], 0)
         arrive(packs_in)
         wide = lanes((cy + 2 * R, cz)) < cz // 2
         for side in range(2):
@@ -306,30 +351,21 @@
                 total = total + zb[side, pl.ds(R + k, cy)] * tap
             pair.append(total)
         pair = rim_pair(pair)
-        for i in range(cx):
-            total = from_rim(pair, i, R)
-            low, mid, high = total[:8], total[8:cy - 8], total[cy - 8:]
-            for k, tap in taps_y:
-                if k >= 0:
-                    low = low + yb[i, pl.ds(R + k, 8)] * tap
-                mid = mid + yb[i, pl.ds(R + 8 + k, cy - 16)] * tap
-                if k <= 0:
-                    high = high + yb[i, pl.ds(R + cy - 8 + k, 8)] * tap
-            co[i] = jnp.concatenate([low, mid, high], 0)
         arrive(late)
         for first in (-8, cy):
-            along_x(first)
+            along_x(first, True, True, False)
             rows = pl.ds(R + first, 8)
             yb[:, rows] = dot(planes(yb, 0, cx, rows), bands[int(flip)]).reshape(cx, 8, cz)
 
         def result(i):
-            low, high = co[i, pl.ds(0, 8)], co[i, pl.ds(cy - 8, 8)]
+            total = co[i] + from_rim(pair, i, R)
+            low, high = total[:8], total[cy - 8:]
             for k, tap in taps_y:
                 if k < 0:
                     low = low + yb[i, pl.ds(R + k, 8)] * tap
                 if k > 0:
                     high = high + yb[i, pl.ds(R + cy - 8 + k, 8)] * tap
-            return jnp.concatenate([low, co[i, pl.ds(8, cy - 16)], high], 0)
+            return jnp.concatenate([low, total[8:cy - 8], high], 0)
 
         return result
 
@@ -345,7 +381,7 @@
         sb[R + i, pl.ds(R, cy)] = source
         packs = pack_one(i, source, packs)
     pack_out(1, packs)
-    start(src_e + src_x + src_z + src_y + src_xy)
+    start(src_x + src_z + src_y + src_xy + src_e)
 
     def z_rim(slot):
         return rim_pair([dot(zin[slot, side, 1, pl.ds(R, cy)], rims[side]) for side in range(2)])
@@ -353,9 +389,10 @@
     def own_part(buf, reach, weight, first_step):
         pair = z_rim(0) if first_step else None
         own = pl.ds(R, cy)
-        for g in range(0, cx, GROUP):
-            along = dot(planes(buf, reach + g, GROUP, own), bands[2])
-            for i in range(g, g + GROUP):
+        step = 2 * GROUP
+        for g in range(0, cx, step):
+            along = dot(planes(buf, reach + g, step, own), bands[2])
+            for i in range(g, g + step):
                 total = buf[reach + i, own] * weight(i) + along[(i - g) * cy:(i - g + 1) * cy]
                 if first_step:
                     total = total + from_rim(pair, i, H)
@@ -491,8 +528,8 @@
         partial = all_sum(partial, sums2, send2.at[1], recv2.at[1], iy, ny, line_id)
     cells = float(cx * cy * cz * nx * ny * nz)
     scale_ref[...] = lax.rsqrt(jnp.full(scale_ref.shape, jnp.sum(partial), jnp.float32) / cells + 1e-06)
-    for copy, to in sent:
-        pl.when(to)(copy.wait_send)
+    for way, (rows, to) in sent_rows.items():
+        pl.when(to)(bytes_of(rows, send.at[way], recv.at[0]).wait_send)
     if near:
         whole.wait_send()
 
@@ -516,9 +553,10 @@
     cx, cy, cz = wave.shape
     nx, ny, nz = sizes
     f32 = jnp.float32
-    n_messages = 72
-    summed = nx * ny * nz if nx <= 4 and ny <= 4 and nz <= 2 else nx * nz
-    most = max(summed, ny)
+    near = nx <= 4 and ny <= 4 and nz <= 2
+    spare_rows = max(2 * (R + H) * cy, 2 * cx * (R + H), 2 * cx * R + 4 * R * R, 6 * cy + 12 * R)
+    summed = nx * ny * nz if near else nx * nz
+    stages, most = (1, 1) if near else (2, max(summed, ny))
     vmem = pl.BlockSpec(memory_space=pltpu.VMEM)
     stay = pl.BlockSpec(memory_space=pltpu.HBM)
     psi, corr, scale = pl.pallas_call(
@@ -540,17 +578,19 @@
             pltpu.VMEM((2, cy + 2 * R, cz), f32),
             pltpu.VMEM((SUBSTEPS - 1, 2, cx // 2, 2 * H, cz), f32),
             pltpu.VMEM((SUBSTEPS - 1, 2, cx // 2, 2 * H, cz), f32),
-            pltpu.VMEM((3, cz, cz), f32),
-            pltpu.VMEM((2, 2, 2 * cz, cz), f32),
-            pltpu.VMEM((2, cz, cz), f32),
+            pltpu.VMEM((3, 2 * cz, 2 * cz), jnp.bfloat16),
+            pltpu.VMEM((2, 2, 4 * cz, 2 * cz), jnp.bfloat16),
+            pltpu.VMEM((2, 2 * cz, 2 * cz), jnp.bfloat16),
+            pltpu.VMEM((cx, cy, cz), f32),
+            pltpu.VMEM((spare_rows, cz), f32),
             pltpu.VMEM((cx, cy, cz), f32),
             pltpu.SMEM(weights.shape, f32),
             pltpu.VMEM((summed, 1, cz), f32),
             pltpu.VMEM((ny, 1, cz), f32),
-            pltpu.SemaphoreType.DMA((n_messages,)),
-            pltpu.SemaphoreType.DMA((n_messages,)),
-            pltpu.SemaphoreType.DMA((2, most)),
-            pltpu.SemaphoreType.DMA((2, most)),
+            pltpu.SemaphoreType.DMA((len(PARTNERS),)),
+            pltpu.SemaphoreType.DMA((6 + SUBSTEPS - 1,)),
+            pltpu.SemaphoreType.DMA((stages, most)),
+            pltpu.SemaphoreType.DMA((stages, most)),
             pltpu.SemaphoreType.DMA((3,)),
         ],
         compiler_params=pltpu.CompilerParams(collective_id=0, has_side_effects=True,

time: 34 us -> 31.6 us (0.929)
  Pallas kernels: 33.2 us -> 30.8 us
    pallas_call x1, Pallas kernels: 32.4 us -> 30 us  [shards(): pl.pallas_call(functools.partial(kernel, sizes), out_shape=(jax.ShapeDtyp...]
where the time goes in v3:
time: 31.6 us; the launch traced here: 31.4 us
  Pallas kernels  30.8 us (97%)
  between operations  0.64 us (2%)
    pallas_call x1, Pallas kernels, shards(): pl.pallas_call(functools.partial(kernel, sizes), out_shape=(jax.ShapeDtyp...  30 us
    pallas_call x1, Pallas kernels, shards(): pl.pallas_call(finish, out_shape=(jax.ShapeDtypeStruct(wave.shape, f32),...  0.81 us

profile of v3, /device:TPU:0, one launch (start us, length us, event | category | flops | bytes accessed | tf_op | source)
XLA Modules:
  0.0 31.4 jit_solution(6758360756235370957)
XLA Ops:
  0.6 30.0 %shard_map.50 = (f32[16,32,128]{2,1,0:T(8,128)S(1)}, f32[16,32,128]{2,1,0:T(8,128)S(1)}, f32[8,128]{1,0:T(8,128)S(1)}) custom-call(f32[3,17]{1,0:T(4,128)} %w_hbm.1, f32[16,32,128]{2,1,0:T(8,128)} %wave_hbm.1, f32[16,32,128]{2,1,0:T(8,128)} %ext_hbm.1), custom_call_target="tpu_custom_call" | custom-call | tf_op jit(solution)/shard_map/pallas_call | solution.py:562
  30.6 0.8 %shard_map.51 = (f32[16,32,128]{2,1,0:T(8,128)}, f32[16,32,128]{2,1,0:T(8,128)}) custom-call(f32[16,32,128]{2,1,0:T(8,128)S(1)} %get-tuple-element.5.psi_ref, f32[16,32,128]{2,1,0:T(8,128)S(1)} %get-tuple-element.6.corr_ref, f32[8,128]{1,0:T(8,128)S(1)} %get-tuple-element.7.scale_ref), custom_call_target="tpu_custom_call" | custom-call | tf_op jit(solution)/shard_map/pallas_call | solution.py:599

commit v4 on v3

--- a/solution.py
+++ b/solution.py
@@ -21,6 +21,7 @@
 
 
 PARTNERS = [(dx, dy, dz) for dx in (-1, 0, 1) for dy in (-1, 0, 1) for dz in (-1, 0, 1) if dx or dy or dz]
+FLAT = [(dx, dy) for dx in (-1, 0, 1) for dy in (-1, 0, 1) if dx or dy]
 GROUP = 4
 
 
@@ -91,6 +92,7 @@
         lax.fori_loop(1, ny, greet(line_id), 0)
 
     blanks[...] = jnp.zeros(blanks.shape, jnp.float32)
+    pool = len(FLAT)
     sent_rows = {}
 
     def rows_of(ref):
@@ -118,19 +120,23 @@
         rows, _ = sent_rows.get(way, (0, to))
         sent_rows[way] = rows + rows_of(dst), to
         copy = pltpu.make_async_remote_copy(
-            src_ref=src, dst_ref=dst, send_sem=send.at[way], recv_sem=recv.at[group],
+            src_ref=src, dst_ref=dst, send_sem=send.at[way],
+            recv_sem=recv.at[group % 2, pool + group // 2 if dz else FLAT.index((dx, dy))],
             device_id=target, device_id_type=MESH)
-        return copy, to, back, dst, group
+        return copy, to, back, dst, dz, group
 
     def start(messages):
         for copy, to, *_ in messages:
             pl.when(to)(copy.start)
 
     def blank(messages):
-        for _, _, back, dst, group in messages:
-            first = [pl.ds(0, n) for n in dst.shape[:-1]]
-            src = blanks.at[tuple(first) if len(first) == 2 else (0, *first)]
-            pl.when(jnp.logical_not(back))(pltpu.make_async_copy(src, dst, recv.at[group]).start)
+        for _, _, back, dst, dz, group in messages:
+            @pl.when(jnp.logical_not(back))
+            def _(dst=dst, dz=dz, group=group):
+                if dz:
+                    pltpu.make_async_copy(blanks.at[pl.ds(0, dst.shape[0])], dst, recv.at[group % 2, pool + group // 2]).start()
+                else:
+                    dst[...] = jnp.zeros(dst.shape, dst.dtype)
 
     def bytes_of(rows, send_sem, recv_sem):
         some = spare.at[pl.ds(0, rows)]
@@ -139,8 +145,14 @@
             device_id={"gx": ix}, device_id_type=MESH)
 
     def arrive(messages):
-        group = messages[0][-1]
-        bytes_of(sum(rows_of(m[3]) for m in messages), send.at[0], recv.at[group]).wait_recv()
+        rows = 0
+        for copy, _, back, dst, dz, group in messages:
+            if dz:
+                rows += rows_of(dst)
+            else:
+                pl.when(back)(copy.wait_recv)
+        if rows:
+            bytes_of(rows, send.at[0], recv.at[group % 2, pool + group // 2]).wait_recv()
 
     at = lanes((cy, cz))
     zero = jnp.zeros((cy, cz), jnp.float32)
@@ -191,34 +203,34 @@
     face_y = [(0, dy) for dy in (1, -1)]
     edge_xy = [(dx, dy) for dx in (1, -1) for dy in (1, -1)]
     src_ref = sb.at[pl.ds(R, cx), pl.ds(R, cy)]
-    wave_x, src_x = side_messages(wave_hbm, wb, face_x, 0), side_messages(src_ref, sb, face_x, 3)
-    wave_y, src_y = side_messages(wave_hbm, wb, face_y, 2), side_messages(src_ref, sb, face_y, 5)
-    wave_xy, src_xy = side_messages(wave_hbm, wb, edge_xy, 2), side_messages(src_ref, sb, edge_xy, 5)
-    wave_z, src_z = z_messages(0, (-1, 0, 1), (0,), 1), z_messages(1, (-1, 0, 1), (0,), 4)
-    wave_e, src_e = z_messages(0, (-1, 0, 1), (-1, 1), 1), z_messages(1, (-1, 0, 1), (-1, 1), 4)
+    wave_x, src_x = side_messages(wave_hbm, wb, face_x, 0), side_messages(src_ref, sb, face_x, 1)
+    wave_y, src_y = side_messages(wave_hbm, wb, face_y, 0), side_messages(src_ref, sb, face_y, 1)
+    wave_xy, src_xy = side_messages(wave_hbm, wb, edge_xy, 0), side_messages(src_ref, sb, edge_xy, 1)
+    wave_z, src_z = z_messages(0, (-1, 0, 1), (0,), 0), z_messages(1, (-1, 0, 1), (0,), 1)
+    wave_e, src_e = z_messages(0, (-1, 0, 1), (-1, 1), 0), z_messages(1, (-1, 0, 1), (-1, 1), 1)
 
     psi_moves = []
     for s in range(SUBSTEPS - 1):
         buf = psi.at[s]
         moves = [
-            message(buf.at[pl.ds(cx, H), pl.ds(R, cy)], buf.at[pl.ds(0, H), pl.ds(R, cy)], 1, 0, 0, 6 + s),
-            message(buf.at[pl.ds(H, H), pl.ds(R, cy)], buf.at[pl.ds(H + cx, H), pl.ds(R, cy)], -1, 0, 0, 6 + s),
+            message(buf.at[pl.ds(cx, H), pl.ds(R, cy)], buf.at[pl.ds(0, H), pl.ds(R, cy)], 1, 0, 0, 2 + s),
+            message(buf.at[pl.ds(H, H), pl.ds(R, cy)], buf.at[pl.ds(H + cx, H), pl.ds(R, cy)], -1, 0, 0, 2 + s),
         ]
         moves += [
-            message(ypack.at[s, 1], yin.at[s, 0], 0, 1, 0, 6 + s),
-            message(ypack.at[s, 0], yin.at[s, 1], 0, -1, 0, 6 + s),
+            message(ypack.at[s, 1], yin.at[s, 0], 0, 1, 0, 2 + s),
+            message(ypack.at[s, 0], yin.at[s, 1], 0, -1, 0, 2 + s),
         ]
-        moves += z_messages(2 + s, (0,), (0,), 6 + s)
+        moves += z_messages(2 + s, (0,), (0,), 2 + s)
         psi_moves.append(moves)
 
     pl.semaphore_wait(barrier, guests)
-    start(wave_x + wave_y + wave_xy)
+    start(wave_x + wave_y)
     get_wave.wait()
     packs = (zero, zero)
     for i in range(cx):
         packs = pack_one(i, wave_ref[i], packs)
     pack_out(0, packs)
-    start(wave_e + wave_z)
+    start(wave_e + wave_z + wave_xy)
     get_ext.start()
     for group in [wave_x, wave_y, wave_xy, wave_z, wave_e, src_x, src_y, src_xy, src_z, src_e] + psi_moves:
         blank(group)
@@ -381,7 +393,7 @@
         sb[R + i, pl.ds(R, cy)] = source
         packs = pack_one(i, source, packs)
     pack_out(1, packs)
-    start(src_x + src_z + src_y + src_xy + src_e)
+    start(src_e + src_z + src_x + src_y + src_xy)
 
     def z_rim(slot):
         return rim_pair([dot(zin[slot, side, 1, pl.ds(R, cy)], rims[side]) for side in range(2)])
@@ -529,7 +541,7 @@
     cells = float(cx * cy * cz * nx * ny * nz)
     scale_ref[...] = lax.rsqrt(jnp.full(scale_ref.shape, jnp.sum(partial), jnp.float32) / cells + 1e-06)
     for way, (rows, to) in sent_rows.items():
-        pl.when(to)(bytes_of(rows, send.at[way], recv.at[0]).wait_send)
+        pl.when(to)(bytes_of(rows, send.at[way], recv.at[0, 0]).wait_send)
     if near:
         whole.wait_send()
 
@@ -581,14 +593,14 @@
             pltpu.VMEM((3, 2 * cz, 2 * cz), jnp.bfloat16),
             pltpu.VMEM((2, 2, 4 * cz, 2 * cz), jnp.bfloat16),
             pltpu.VMEM((2, 2 * cz, 2 * cz), jnp.bfloat16),
-            pltpu.VMEM((cx, cy, cz), f32),
+            pltpu.VMEM((cy, cz), f32),
             pltpu.VMEM((spare_rows, cz), f32),
             pltpu.VMEM((cx, cy, cz), f32),
             pltpu.SMEM(weights.shape, f32),
             pltpu.VMEM((summed, 1, cz), f32),
             pltpu.VMEM((ny, 1, cz), f32),
             pltpu.SemaphoreType.DMA((len(PARTNERS),)),
-            pltpu.SemaphoreType.DMA((6 + SUBSTEPS - 1,)),
+            pltpu.SemaphoreType.DMA((2, len(FLAT) + 1 + SUBSTEPS // 2)),
             pltpu.SemaphoreType.DMA((stages, most)),
             pltpu.SemaphoreType.DMA((stages, most)),
             pltpu.SemaphoreType.DMA((3,)),

time: 31.6 us -> 30.3 us (0.959)
  Pallas kernels: 30.8 us -> 29.5 us
    pallas_call x1, Pallas kernels: 30 us -> 28.7 us  [shards(): pl.pallas_call(functools.partial(kernel, sizes), out_shape=(jax.ShapeDtyp...]
where the time goes in v4:
time: 30.3 us; the launch traced here: 30.1 us
  Pallas kernels  29.5 us (97%)
  between operations  0.64 us (2%)
    pallas_call x1, Pallas kernels, shards(): pl.pallas_call(functools.partial(kernel, sizes), out_shape=(jax.ShapeDtyp...  28.7 us
    pallas_call x1, Pallas kernels, shards(): pl.pallas_call(finish, out_shape=(jax.ShapeDtypeStruct(wave.shape, f32),...  0.81 us

profile of v4, /device:TPU:0, one launch (start us, length us, event | category | flops | bytes accessed | tf_op | source)
XLA Modules:
  0.0 30.1 jit_solution(8622902787896870053)
XLA Ops:
  0.6 28.7 %shard_map.50 = (f32[16,32,128]{2,1,0:T(8,128)S(1)}, f32[16,32,128]{2,1,0:T(8,128)S(1)}, f32[8,128]{1,0:T(8,128)S(1)}) custom-call(f32[3,17]{1,0:T(4,128)} %w_hbm.1, f32[16,32,128]{2,1,0:T(8,128)} %wave_hbm.1, f32[16,32,128]{2,1,0:T(8,128)} %ext_hbm.1), custom_call_target="tpu_custom_call" | custom-call | tf_op jit(solution)/shard_map/pallas_call | solution.py:574
  29.3 0.8 %shard_map.51 = (f32[16,32,128]{2,1,0:T(8,128)}, f32[16,32,128]{2,1,0:T(8,128)}) custom-call(f32[16,32,128]{2,1,0:T(8,128)S(1)} %get-tuple-element.5.psi_ref, f32[16,32,128]{2,1,0:T(8,128)S(1)} %get-tuple-element.6.corr_ref, f32[8,128]{1,0:T(8,128)S(1)} %get-tuple-element.7.scale_ref), custom_call_target="tpu_custom_call" | custom-call | tf_op jit(solution)/shard_map/pallas_call | solution.py:611

commit v5 on v4

--- a/solution.py
+++ b/solution.py
@@ -21,6 +21,7 @@
 
 
 PARTNERS = [(dx, dy, dz) for dx in (-1, 0, 1) for dy in (-1, 0, 1) for dz in (-1, 0, 1) if dx or dy or dz]
+PARTNERS.sort(key=lambda d: d.count(0))
 FLAT = [(dx, dy) for dx in (-1, 0, 1) for dy in (-1, 0, 1) if dx or dy]
 GROUP = 4
 
@@ -34,7 +35,7 @@
 
 
 def kernel(sizes, w_hbm, wave_hbm, ext_hbm, out_ref, corr_ref, scale_ref,
-           wb, sb, yb, co, psi, va, part, pack, zin, zb, ypack, yin, bands, edges, rims, blanks, spare, ext_ref, w_ref,
+           wb, sb, yb, co, psi, va, part, pack, zin, zb, ypack, yin, bands, edges, blanks, spill, spare, ext_ref, w_ref,
            sums, sums2, send, recv, send2, recv2, local):
     nx, ny, nz = sizes
     cx, cy, cz = wave_hbm.shape
@@ -91,9 +92,13 @@
         lax.fori_loop(1, plane, greet(plane_id), 0)
         lax.fori_loop(1, ny, greet(line_id), 0)
 
+    everyone = plane * ny
+    order = (ix * ny + iy) * nz + iz
+    others = [jnp.where(order + d < everyone, order + d, order + d - everyone) for d in range(1, everyone)] if near else []
     blanks[...] = jnp.zeros(blanks.shape, jnp.float32)
     pool = len(FLAT)
     sent_rows = {}
+    spilled = [0]
 
     def rows_of(ref):
         count = 1
@@ -116,21 +121,27 @@
         for name, d, i, n in zip(AXES, (dx, dy, dz), (ix, iy, iz), sizes):
             if d:
                 target[name] = jnp.clip(i + d, 0, n - 1)
-        way = PARTNERS.index((dx, dy, dz))
-        rows, _ = sent_rows.get(way, (0, to))
-        sent_rows[way] = rows + rows_of(dst), to
+        way = pool if dz else FLAT.index((dx, dy))
+        rows, _ = sent_rows.get(way, (0, None))
+        sent_rows[way] = rows + rows_of(dst), None if dz else to
         copy = pltpu.make_async_remote_copy(
             src_ref=src, dst_ref=dst, send_sem=send.at[way],
-            recv_sem=recv.at[group % 2, pool + group // 2 if dz else FLAT.index((dx, dy))],
+            recv_sem=recv.at[group % 2, pool + group // 2 if dz else way],
             device_id=target, device_id_type=MESH)
-        return copy, to, back, dst, dz, group
+        return copy, to, back, dst, dz, group, way
 
     def start(messages):
         for copy, to, *_ in messages:
             pl.when(to)(copy.start)
 
     def blank(messages):
-        for _, _, back, dst, dz, group in messages:
+        for _, to, back, dst, dz, group, _ in messages:
+            if dz:
+                some = pl.ds(0, dst.shape[0])
+                waste = spill.at[pl.ds(spilled[0], dst.shape[0])]
+                spilled[0] += dst.shape[0]
+                pl.when(jnp.logical_not(to))(pltpu.make_async_copy(blanks.at[some], waste, send.at[pool]).start)
+
             @pl.when(jnp.logical_not(back))
             def _(dst=dst, dz=dz, group=group):
                 if dz:
@@ -145,23 +156,25 @@
             device_id={"gx": ix}, device_id_type=MESH)
 
     def arrive(messages):
-        rows = 0
-        for copy, _, back, dst, dz, group in messages:
-            if dz:
-                rows += rows_of(dst)
+        rows, waits = {}, {}
+        for _, _, back, dst, dz, group, way in messages:
+            rows[way] = rows.get(way, 0) + rows_of(dst)
+            waits[way] = None if dz else back, recv.at[group % 2, way + group // 2 if dz else way]
+        for way, (back, sem) in waits.items():
+            wait = bytes_of(rows[way], send.at[0], sem).wait_recv
+            if back is None:
+                wait()
             else:
-                pl.when(back)(copy.wait_recv)
-        if rows:
-            bytes_of(rows, send.at[0], recv.at[group % 2, pool + group // 2]).wait_recv()
+                pl.when(back)(wait)
 
     at = lanes((cy, cz))
     zero = jnp.zeros((cy, cz), jnp.float32)
 
+    slot_of = lax.div(at, per)
+
     def pack_one(i, value, packs):
-        mine = (at >= per * i) & (at < per * i + per)
-        low = turn(value, per * i)
-        high = turn(value, modulo(per * i + per, cz))
-        return jnp.where(mine, low, packs[0]), jnp.where(mine, high, packs[1])
+        moved = turn(value, modulo(per * i, cz))
+        return jnp.where(slot_of == i, moved, packs[0]), jnp.where(slot_of == (i - 1) % cx, moved, packs[1])
 
     def pack_out(slot, packs):
         pack[slot, 0] = packs[0]
@@ -181,7 +194,7 @@
                 out.append(message(pack.at[slot, 0, rows], zin.at[slot, 1, 1 - dx, into], dx, dy, -1, group))
         return out
 
-    def side_messages(src, dst, moves, group):
+    def side_messages(src, dst, moves, group, part=0, parts=1):
         out = []
         for dx, dy in moves:
             if dx > 0:
@@ -189,13 +202,15 @@
             elif dx < 0:
                 sx, tx = pl.ds(0, R), pl.ds(R + cx, R)
             else:
-                sx, tx = pl.ds(0, cx), pl.ds(R, cx)
+                some = cx // parts
+                sx, tx = pl.ds(part * some, some), pl.ds(R + part * some, some)
             if dy > 0:
                 sy, ty = pl.ds(cy - R, R), pl.ds(0, R)
             elif dy < 0:
                 sy, ty = pl.ds(0, R), pl.ds(R + cy, R)
             else:
-                sy, ty = pl.ds(0, cy), pl.ds(R, cy)
+                some = cy // parts
+                sy, ty = pl.ds(part * some, some), pl.ds(R + part * some, some)
             out.append(message(src.at[sx, sy], dst.at[tx, ty], dx, dy, 0, group))
         return out
 
@@ -203,8 +218,9 @@
     face_y = [(0, dy) for dy in (1, -1)]
     edge_xy = [(dx, dy) for dx in (1, -1) for dy in (1, -1)]
     src_ref = sb.at[pl.ds(R, cx), pl.ds(R, cy)]
-    wave_x, src_x = side_messages(wave_hbm, wb, face_x, 0), side_messages(src_ref, sb, face_x, 1)
-    wave_y, src_y = side_messages(wave_hbm, wb, face_y, 0), side_messages(src_ref, sb, face_y, 1)
+    wave_x1, wave_x2 = (side_messages(wave_hbm, wb, face_x, 0, n, 2) for n in range(2))
+    wave_y1, wave_y2 = (side_messages(wave_hbm, wb, face_y, 0, n, 2) for n in range(2))
+    src_x, src_y = side_messages(src_ref, sb, face_x, 1), side_messages(src_ref, sb, face_y, 1)
     wave_xy, src_xy = side_messages(wave_hbm, wb, edge_xy, 0), side_messages(src_ref, sb, edge_xy, 1)
     wave_z, src_z = z_messages(0, (-1, 0, 1), (0,), 0), z_messages(1, (-1, 0, 1), (0,), 1)
     wave_e, src_e = z_messages(0, (-1, 0, 1), (-1, 1), 0), z_messages(1, (-1, 0, 1), (-1, 1), 1)
@@ -224,13 +240,14 @@
         psi_moves.append(moves)
 
     pl.semaphore_wait(barrier, guests)
-    start(wave_x + wave_y)
+    start(wave_x1 + wave_y1)
     get_wave.wait()
     packs = (zero, zero)
     for i in range(cx):
         packs = pack_one(i, wave_ref[i], packs)
     pack_out(0, packs)
-    start(wave_e + wave_z + wave_xy)
+    start(wave_e + wave_z + wave_x2 + wave_y2 + wave_xy)
+    wave_x, wave_y = wave_x1 + wave_x2, wave_y1 + wave_y2
     get_ext.start()
     for group in [wave_x, wave_y, wave_xy, wave_z, wave_e, src_x, src_y, src_xy, src_z, src_e] + psi_moves:
         blank(group)
@@ -288,17 +305,15 @@
             is_owner = [owner[side] == q for q in range(cx)]
             rows = []
             for t in range(2 * cx):
-                at_plane = t if t < cx else (t if t - cx < cx // 2 else t - 2 * cx)
+                at_plane = (t + 1 - side) % cx
+                if t >= cx:
+                    at_plane += cx if at_plane < cx // 2 else -cx
                 by_x = none
                 for q in range(cx):
                     if at_plane - q in taps:
                         by_x = jnp.where(is_owner[q], taps[at_plane - q], by_x)
                 rows.append(by_x * by_z)
             keep(edges, (flip, side), jnp.concatenate(rows, 0))
-    for side in range(2):
-        by_z = corner(side, [(k, tap) for k, tap in z_taps[2] if (k < 0) == (side == 0)])
-        keep(rims, (side,), jnp.concatenate([jnp.where(owner[side] == t, by_z, none) for t in range(cx)], 0))
-
     even = lax.rem(lax.div(at, per), 2) == 0
 
     def rim_pair(sides):
@@ -349,8 +364,9 @@
                     high = a if high is None else high + a
             co[i] = jnp.concatenate([low, mid, high], 0)
         arrive(packs_in)
-        wide = lanes((cy + 2 * R, cz)) < cz // 2
+        wide_slot = lax.div(lanes((cy + 2 * R, cz)), per)
         for side in range(2):
+            wide = lax.rem(wide_slot + 1 - side, cx) < cx // 2
             mine = zin[slot, side, 1]
             other = jnp.where(wide, zin[slot, side, 2], zin[slot, side, 0])
             if square:
@@ -395,8 +411,15 @@
     pack_out(1, packs)
     start(src_e + src_z + src_x + src_y + src_xy)
 
+    cell_of = lax.rem(at, per)
+
     def z_rim(slot):
-        return rim_pair([dot(zin[slot, side, 1, pl.ds(R, cy)], rims[side]) for side in range(2)])
+        low, high = (zin[slot, side, 1, pl.ds(R, cy)] for side in range(2))
+        made = [zero, zero]
+        for k in range(1, H + 1):
+            made[0] = made[0] + gains[k] * jnp.where(cell_of < k, turn(low, k), zero)
+            made[1] = made[1] + gains[k] * jnp.where(cell_of >= per - k, turn(high, cz - k), zero)
+        return rim_pair(made)
 
     def own_part(buf, reach, weight, first_step):
         pair = z_rim(0) if first_step else None
@@ -426,7 +449,7 @@
                 part[i] = total
 
     def halo_part(buf, pair, i):
-        total = part[i] + from_rim(pair, i, H)
+        total = part[i]
         for k in range(1, H + 1):
             for j in (i - k, i + k):
                 if not 0 <= j < cx:
@@ -435,7 +458,7 @@
         for k in range(1, H + 1):
             low = low + gains[k] * buf[H + i, pl.ds(R - k, 8)]
             high = high + gains[k] * buf[H + i, pl.ds(R + cy - 8 + k, 8)]
-        return jnp.concatenate([low, total[8:cy - 8], high], 0)
+        return jnp.concatenate([low, total[8:cy - 8], high], 0) + from_rim(pair, i, H)
 
     middle = 1.0 + STEP * 0.5 * 3.0 * LAP_COEF[0]
     own_part(wb, R, lambda i: middle, True)
@@ -473,11 +496,11 @@
         buf = psi.at[s]
         own_part(buf, H, lambda i: va[i], False)
         arrive(psi_moves[s])
+        pair = z_rim(2 + s)
         for i in range(cx):
             half = pl.ds(H * (i % 2), H)
             buf[H + i, pl.ds(R - H, H)] = yin[s, 0, i // 2, half]
             buf[H + i, pl.ds(R + cy, H)] = yin[s, 1, i // 2, half]
-        pair = z_rim(2 + s)
         if s < SUBSTEPS - 2:
             send_out(s + 1, lambda i: halo_part(buf, pair, i))
         else:
@@ -487,14 +510,6 @@
                 total = total + value * value
 
     partial = jnp.sum(total, axis=0, keepdims=True)
-    everyone = plane * ny
-    me = iy * plane + here
-
-    def any_id(d):
-        t = lax.rem(me + d, everyone)
-        p = lax.rem(t, plane)
-        return t, {"gx": lax.div(p, nz), "gy": lax.div(t, plane), "gz": lax.rem(p, nz)}
-
     def all_sum(value, slots, ssem, rsem, me, n, ids):
         if n == 1:
             return value
@@ -528,20 +543,24 @@
         for d in range(1, everyone):
             pltpu.make_async_remote_copy(
                 src_ref=sums.at[0], dst_ref=sums.at[d], send_sem=send2.at[0, 0], recv_sem=recv2.at[0, 0],
-                device_id=any_id(d)[1], device_id_type=MESH).start()
+                device_id=others[d - 1], device_id_type=pl.DeviceIdType.LOGICAL).start()
         rest = sums.at[pl.ds(1, everyone - 1)]
         whole = pltpu.make_async_remote_copy(
             src_ref=rest, dst_ref=rest, send_sem=send2.at[0, 0], recv_sem=recv2.at[0, 0],
-            device_id=any_id(1)[1], device_id_type=MESH)
+            device_id=others[0], device_id_type=pl.DeviceIdType.LOGICAL)
         whole.wait_recv()
         partial = jnp.sum(sums[...], axis=0)
     else:
         partial = all_sum(partial, sums, send2.at[0], recv2.at[0], here, plane, plane_id)
         partial = all_sum(partial, sums2, send2.at[1], recv2.at[1], iy, ny, line_id)
     cells = float(cx * cy * cz * nx * ny * nz)
-    scale_ref[...] = lax.rsqrt(jnp.full(scale_ref.shape, jnp.sum(partial), jnp.float32) / cells + 1e-06)
+    scale_ref[...] = lax.rsqrt(jnp.broadcast_to(jnp.sum(partial, axis=1, keepdims=True), scale_ref.shape) / cells + 1e-06)
     for way, (rows, to) in sent_rows.items():
-        pl.when(to)(bytes_of(rows, send.at[way], recv.at[0, 0]).wait_send)
+        left = bytes_of(rows, send.at[way], recv.at[0, 0]).wait_send
+        if to is None:
+            left()
+        else:
+            pl.when(to)(left)
     if near:
         whole.wait_send()
 
@@ -566,7 +585,7 @@
     nx, ny, nz = sizes
     f32 = jnp.float32
     near = nx <= 4 and ny <= 4 and nz <= 2
-    spare_rows = max(2 * (R + H) * cy, 2 * cx * (R + H), 2 * cx * R + 4 * R * R, 6 * cy + 12 * R)
+    spare_rows = max(2 * (R + H) * cy, 2 * cx * (R + H), 2 * cx * R + 4 * R * R, 6 * cy + 12 * R, 2 * (6 * cy + 12 * R) + 4 * cy)
     summed = nx * ny * nz if near else nx * nz
     stages, most = (1, 1) if near else (2, max(summed, ny))
     vmem = pl.BlockSpec(memory_space=pltpu.VMEM)
@@ -592,14 +611,14 @@
             pltpu.VMEM((SUBSTEPS - 1, 2, cx // 2, 2 * H, cz), f32),
             pltpu.VMEM((3, 2 * cz, 2 * cz), jnp.bfloat16),
             pltpu.VMEM((2, 2, 4 * cz, 2 * cz), jnp.bfloat16),
-            pltpu.VMEM((2, 2 * cz, 2 * cz), jnp.bfloat16),
             pltpu.VMEM((cy, cz), f32),
+            pltpu.VMEM((2 * (6 * cy + 12 * R) + 2 * (SUBSTEPS - 1) * cy, cz), f32),
             pltpu.VMEM((spare_rows, cz), f32),
             pltpu.VMEM((cx, cy, cz), f32),
             pltpu.SMEM(weights.shape, f32),
             pltpu.VMEM((summed, 1, cz), f32),
             pltpu.VMEM((ny, 1, cz), f32),
-            pltpu.SemaphoreType.DMA((len(PARTNERS),)),
+            pltpu.SemaphoreType.DMA((len(FLAT) + 1,)),
             pltpu.SemaphoreType.DMA((2, len(FLAT) + 1 + SUBSTEPS // 2)),
             pltpu.SemaphoreType.DMA((stages, most)),
             pltpu.SemaphoreType.DMA((stages, most)),

time: 30.3 us -> 29.9 us (0.987)
  Pallas kernels: 29.5 us -> 29.1 us
    pallas_call x1, Pallas kernels: 28.7 us -> 28.3 us  [shards(): pl.pallas_call(functools.partial(kernel, sizes), out_shape=(jax.ShapeDtyp...]
where the time goes in v5:
time: 29.9 us; the launch traced here: 29.7 us
  Pallas kernels  29.1 us (97%)
  between operations  0.64 us (2%)
    pallas_call x1, Pallas kernels, shards(): pl.pallas_call(functools.partial(kernel, sizes), out_shape=(jax.ShapeDtyp...  28.3 us
    pallas_call x1, Pallas kernels, shards(): pl.pallas_call(finish, out_shape=(jax.ShapeDtypeStruct(wave.shape, f32),...  0.81 us

profile of v5, /device:TPU:0, one launch (start us, length us, event | category | flops | bytes accessed | tf_op | source)
XLA Modules:
  0.0 29.7 jit_solution(18254772512725625370)
XLA Ops:
  0.6 28.3 %shard_map.50 = (f32[16,32,128]{2,1,0:T(8,128)S(1)}, f32[16,32,128]{2,1,0:T(8,128)S(1)}, f32[8,128]{1,0:T(8,128)S(1)}) custom-call(f32[3,17]{1,0:T(4,128)} %w_hbm.1, f32[16,32,128]{2,1,0:T(8,128)} %wave_hbm.1, f32[16,32,128]{2,1,0:T(8,128)} %ext_hbm.1), custom_call_target="tpu_custom_call" | custom-call | tf_op jit(solution)/shard_map/pallas_call | solution.py:593
  28.9 0.8 %shard_map.51 = (f32[16,32,128]{2,1,0:T(8,128)}, f32[16,32,128]{2,1,0:T(8,128)}) custom-call(f32[16,32,128]{2,1,0:T(8,128)S(1)} %get-tuple-element.5.psi_ref, f32[16,32,128]{2,1,0:T(8,128)S(1)} %get-tuple-element.6.corr_ref, f32[8,128]{1,0:T(8,128)S(1)} %get-tuple-element.7.scale_ref), custom_call_target="tpu_custom_call" | custom-call | tf_op jit(solution)/shard_map/pallas_call | solution.py:630

commit v6 on v5

--- a/solution.py
+++ b/solution.py
@@ -35,7 +35,7 @@
 
 
 def kernel(sizes, w_hbm, wave_hbm, ext_hbm, out_ref, corr_ref, scale_ref,
-           wb, sb, yb, co, psi, va, part, pack, zin, zb, ypack, yin, bands, edges, blanks, spill, spare, ext_ref, w_ref,
+           wb, sb, yb, co, pb, psi, va, part, pack, zin, zb, vx, ypack, yin, bands, edges, blanks, spill, spare, ext_ref, w_ref,
            sums, sums2, send, recv, send2, recv2, local):
     nx, ny, nz = sizes
     cx, cy, cz = wave_hbm.shape
@@ -194,13 +194,13 @@
                 out.append(message(pack.at[slot, 0, rows], zin.at[slot, 1, 1 - dx, into], dx, dy, -1, group))
         return out
 
-    def side_messages(src, dst, moves, group, part=0, parts=1):
+    def side_messages(src, dst, moves, group, part=0, parts=1, wide=R):
         out = []
         for dx, dy in moves:
             if dx > 0:
-                sx, tx = pl.ds(cx - R, R), pl.ds(0, R)
+                sx, tx = pl.ds(cx - wide, wide), pl.ds(R - wide, wide)
             elif dx < 0:
-                sx, tx = pl.ds(0, R), pl.ds(R + cx, R)
+                sx, tx = pl.ds(0, wide), pl.ds(R + cx, wide)
             else:
                 some = cx // parts
                 sx, tx = pl.ds(part * some, some), pl.ds(R + part * some, some)
@@ -225,19 +225,17 @@
     wave_z, src_z = z_messages(0, (-1, 0, 1), (0,), 0), z_messages(1, (-1, 0, 1), (0,), 1)
     wave_e, src_e = z_messages(0, (-1, 0, 1), (-1, 1), 0), z_messages(1, (-1, 0, 1), (-1, 1), 1)
 
-    psi_moves = []
-    for s in range(SUBSTEPS - 1):
-        buf = psi.at[s]
-        moves = [
-            message(buf.at[pl.ds(cx, H), pl.ds(R, cy)], buf.at[pl.ds(0, H), pl.ds(R, cy)], 1, 0, 0, 2 + s),
-            message(buf.at[pl.ds(H, H), pl.ds(R, cy)], buf.at[pl.ds(H + cx, H), pl.ds(R, cy)], -1, 0, 0, 2 + s),
-        ]
-        moves += [
-            message(ypack.at[s, 1], yin.at[s, 0], 0, 1, 0, 2 + s),
-            message(ypack.at[s, 0], yin.at[s, 1], 0, -1, 0, 2 + s),
-        ]
-        moves += z_messages(2 + s, (0,), (0,), 2 + s)
-        psi_moves.append(moves)
+    own_psi = pb.at[pl.ds(R, cx), pl.ds(R, cy)]
+    psi_x = side_messages(own_psi, pb, face_x, 2) + [
+        message(va.at[pl.ds(cx - H, H)], vx.at[0], 1, 0, 0, 2),
+        message(va.at[pl.ds(0, H)], vx.at[1], -1, 0, 0, 2),
+    ]
+    psi_y = side_messages(own_psi, pb, face_y, 2) + [
+        message(ypack.at[1], yin.at[0], 0, 1, 0, 2),
+        message(ypack.at[0], yin.at[1], 0, -1, 0, 2),
+    ] + side_messages(own_psi, pb, edge_xy, 2, wide=H)
+    psi_z = z_messages(2, (-1, 0, 1), (0,), 2) + z_messages(2, (0,), (-1, 1), 2) + z_messages(3, (0,), (0,), 2)
+    psi_moves = psi_z + psi_x + psi_y
 
     pl.semaphore_wait(barrier, guests)
     start(wave_x1 + wave_y1)
@@ -249,7 +247,7 @@
     start(wave_e + wave_z + wave_x2 + wave_y2 + wave_xy)
     wave_x, wave_y = wave_x1 + wave_x2, wave_y1 + wave_y2
     get_ext.start()
-    for group in [wave_x, wave_y, wave_xy, wave_z, wave_e, src_x, src_y, src_xy, src_z, src_e] + psi_moves:
+    for group in [wave_x, wave_y, wave_xy, wave_z, wave_e, src_x, src_y, src_xy, src_z, src_e, psi_moves]:
         blank(group)
     get_weights.wait()
 
@@ -314,13 +312,14 @@
                         by_x = jnp.where(is_owner[q], taps[at_plane - q], by_x)
                 rows.append(by_x * by_z)
             keep(edges, (flip, side), jnp.concatenate(rows, 0))
-    even = lax.rem(lax.div(at, per), 2) == 0
-
     def rim_pair(sides):
+        even = lax.rem(lax.div(lanes(sides[0].shape), per), 2) == 0
         return jnp.where(even, sides[0], sides[1]), jnp.where(even, sides[1], sides[0])
 
     def from_rim(pair, i, width):
-        return jnp.where((at < width) | (at >= cz - width), turn(pair[i % 2], modulo(cz - per * i, cz)), zero)
+        spot = lanes(pair[0].shape)
+        moved = turn(pair[i % 2], modulo(cz - per * i, cz))
+        return jnp.where((spot < width) | (spot >= cz - width), moved, jnp.zeros_like(moved))
 
     def planes(buf, first, count, rows):
         return buf[pl.ds(first, count), rows].reshape(count * rows.size, cz)
@@ -411,15 +410,16 @@
     pack_out(1, packs)
     start(src_e + src_z + src_x + src_y + src_xy)
 
-    cell_of = lax.rem(at, per)
-
-    def z_rim(slot):
-        low, high = (zin[slot, side, 1, pl.ds(R, cy)] for side in range(2))
-        made = [zero, zero]
+    def z_rim_of(low, high):
+        cell_of = lax.rem(lanes(low.shape), per)
+        made = [jnp.zeros_like(low), jnp.zeros_like(low)]
         for k in range(1, H + 1):
-            made[0] = made[0] + gains[k] * jnp.where(cell_of < k, turn(low, k), zero)
-            made[1] = made[1] + gains[k] * jnp.where(cell_of >= per - k, turn(high, cz - k), zero)
+            made[0] = made[0] + gains[k] * jnp.where(cell_of < k, turn(low, k), 0.0)
+            made[1] = made[1] + gains[k] * jnp.where(cell_of >= per - k, turn(high, cz - k), 0.0)
         return rim_pair(made)
+
+    def z_rim(slot, place=1, rows=pl.ds(R, cy)):
+        return z_rim_of(*[zin[slot, side, place, rows] for side in range(2)])
 
     def own_part(buf, reach, weight, first_step):
         pair = z_rim(0) if first_step else None
@@ -448,66 +448,107 @@
                     total = total + jnp.concatenate([up[:8], up[8:] + down[:cy - 16], down[cy - 16:]], 0)
                 part[i] = total
 
-    def halo_part(buf, pair, i):
+    def halo_part(buf, reach, pair, i):
         total = part[i]
         for k in range(1, H + 1):
             for j in (i - k, i + k):
                 if not 0 <= j < cx:
-                    total = total + gains[k] * buf[H + j, pl.ds(R, cy)]
+                    total = total + gains[k] * buf[reach + j, pl.ds(R, cy)]
         low, high = total[:8], total[cy - 8:]
         for k in range(1, H + 1):
-            low = low + gains[k] * buf[H + i, pl.ds(R - k, 8)]
-            high = high + gains[k] * buf[H + i, pl.ds(R + cy - 8 + k, 8)]
+            low = low + gains[k] * buf[reach + i, pl.ds(R - k, 8)]
+            high = high + gains[k] * buf[reach + i, pl.ds(R + cy - 8 + k, 8)]
         return jnp.concatenate([low, total[8:cy - 8], high], 0) + from_rim(pair, i, H)
 
     middle = 1.0 + STEP * 0.5 * 3.0 * LAP_COEF[0]
     own_part(wb, R, lambda i: middle, True)
     smeared = smear(sb, 1, False, True, src_x, src_z + src_e, src_y + src_xy)
     get_ext.wait()
-    groups = [list(range(g, g + GROUP)) for g in range(0, cx, GROUP)]
-    groups = groups[:1] + groups[-1:] + groups[1:-1]
-
-    def first_step(i):
+    psi_packs = va_packs = (zero, zero)
+    for i in range(cx):
         corr = corr_ref[i] + smeared(i)
         corr_ref[i] = corr
         felt = STEP * (corr + ext_ref[i])
-        va[i] = middle - felt
-        return part[i] - felt * wave_ref[i]
-
-    def send_out(s, step):
-        after = psi.at[s]
-        packs = (zero, zero)
-        for n_, these in enumerate(groups):
-            for i in these:
-                value = step(i)
-                after[H + i, pl.ds(R, cy)] = value
-                packs = pack_one(i, value, packs)
-                half = pl.ds(H * (i % 2), H)
-                ypack[s, 0, i // 2, half] = value[:H]
-                ypack[s, 1, i // 2, half] = value[cy - H:]
-            if n_ == 1:
-                start(psi_moves[s][:2])
-        pack_out(2 + s, packs)
-        start(psi_moves[s][2:])
-
-    send_out(0, first_step)
+        weight = middle - felt
+        va[i] = weight
+        value = part[i] - felt * wave_ref[i]
+        pb[R + i, pl.ds(R, cy)] = value
+        psi_packs = pack_one(i, value, psi_packs)
+        va_packs = pack_one(i, weight, va_packs)
+        half = pl.ds(H * (i % 2), H)
+        ypack[0, i // 2, half] = weight[:H]
+        ypack[1, i // 2, half] = weight[cy - H:]
+    pack_out(2, psi_packs)
+    pack_out(3, va_packs)
+    start(psi_moves)
+    own_part(pb, R, lambda i: va[i], False)
+    arrive(psi_moves)
+    own = pl.ds(R, cy)
+    inside = {(0, 0): ix > 0, (0, 1): ix < nx - 1, (1, 0): iy > 0, (1, 1): iy < ny - 1, (2, 0): iz > 0, (2, 1): iz < nz - 1}
+
+    def kept(dim, side, value):
+        return jnp.where(inside[dim, side], value, 0.0)
+
+    def star(p, first, rows):
+        total = None
+        for k in range(1, H + 1):
+            pairs = pb[R + p - k, pl.ds(first, rows)] + pb[R + p + k, pl.ds(first, rows)]
+            pairs += pb[R + p, pl.ds(first - k, rows)] + pb[R + p, pl.ds(first + k, rows)]
+            total = gains[k] * pairs if total is None else total + gains[k] * pairs
+        return total
+
+    for side in range(2):
+        pair = z_rim(2, 2 * side)
+        begin = cx if side else -H
+        along = dot(planes(pb, R + begin, H, own), bands[2])
+        for n in range(H):
+            p = begin + n
+            total = pb[R + p, own] * vx[side, n] + along[n * cy:(n + 1) * cy] + star(p, R, cy)
+            psi[H + p, own] = kept(0, side, total + from_rim(pair, p % cx, H))
+    for side in range(2):
+        first = R + cy - H if side else R - H
+        pair = z_rim(2, 1, pl.ds(first, 2 * H))
+        centers = [pb[R + i, pl.ds(first, 2 * H)] for i in range(cx)]
+        along = dot(jnp.concatenate(centers, 0), bands[2])
+        for i in range(cx):
+            weight = yin[side, i // 2]
+            if i % 2 != side:
+                weight = pltpu.roll(weight, H, 0)
+            total = centers[i] * weight + along[i * 2 * H:(i + 1) * 2 * H] + star(i, first, 2 * H)
+            total = kept(1, side, total + from_rim(pair, i, H))
+            if side:
+                psi[H + i, pl.ds(R + cy, H)] = total[H:]
+            else:
+                psi[H + i, pl.ds(R - H, H)] = total[:H]
+    rim = []
+    cell = lax.rem(at, per)
+    for side in range(2):
+        far = zin[2, side, 1, own]
+        plane_at = lax.rem(slot_of + 1 - side, cx)
+        mine = turn(pack[2, side], per if side else cz - per)
+        total = far * zin[3, side, 1, own]
+        for k in range(1, H + 1):
+            ahead = turn(jnp.where(plane_at < k, zin[2, side, 2, own], far), cz - per * k)
+            behind = turn(jnp.where(plane_at >= cx - k, zin[2, side, 0, own], far), per * k)
+            up, down = turn(far, cz - k), turn(far, k)
+            if side:
+                down = jnp.where(cell >= k, down, turn(mine, cz - per + k))
+            else:
+                up = jnp.where(cell < per - k, up, turn(mine, per - k))
+            pairs = ahead + behind + up + down
+            pairs += zin[2, side, 1, pl.ds(R - k, cy)] + zin[2, side, 1, pl.ds(R + k, cy)]
+            total = total + gains[k] * pairs
+        rim.append(kept(2, side, total))
+    pair = z_rim(2)
+    for i in range(cx):
+        psi[H + i, own] = halo_part(pb, R, pair, i)
+    own_part(psi, H, lambda i: va[i], False)
+    pair = z_rim_of(*rim)
     total = zero
-    for s in range(SUBSTEPS - 1):
-        buf = psi.at[s]
-        own_part(buf, H, lambda i: va[i], False)
-        arrive(psi_moves[s])
-        pair = z_rim(2 + s)
-        for i in range(cx):
-            half = pl.ds(H * (i % 2), H)
-            buf[H + i, pl.ds(R - H, H)] = yin[s, 0, i // 2, half]
-            buf[H + i, pl.ds(R + cy, H)] = yin[s, 1, i // 2, half]
-        if s < SUBSTEPS - 2:
-            send_out(s + 1, lambda i: halo_part(buf, pair, i))
-        else:
-            for i in range(cx):
-                value = halo_part(buf, pair, i)
-                out_ref[i] = value
-                total = total + value * value
+    for i in range(cx):
+        value = halo_part(psi, H, pair, i)
+        out_ref[i] = value
+        total = total + value * value
 
     partial = jnp.sum(total, axis=0, keepdims=True)
     def all_sum(value, slots, ssem, rsem, me, n, ids):
@@ -585,7 +626,7 @@
     nx, ny, nz = sizes
     f32 = jnp.float32
     near = nx <= 4 and ny <= 4 and nz <= 2
-    spare_rows = max(2 * (R + H) * cy, 2 * cx * (R + H), 2 * cx * R + 4 * R * R, 6 * cy + 12 * R, 2 * (6 * cy + 12 * R) + 4 * cy)
+    spare_rows = max(2 * (R + H) * cy, 2 * cx * (R + H), 2 * cx * R + 4 * R * R, 6 * cy + 12 * R, 2 * (6 * cy + 12 * R) + 8 * cy + 4 * R, (3 * R + H) * cy, 3 * cx * R + cx * H)
     summed = nx * ny * nz if near else nx * nz
     stages, most = (1, 1) if near else (2, max(summed, ny))
     vmem = pl.BlockSpec(memory_space=pltpu.VMEM)
@@ -601,25 +642,27 @@
             pltpu.VMEM((cx + 2 * R, cy + 2 * R, cz), f32),
             pltpu.VMEM((cx, cy + 2 * R, cz), f32),
             pltpu.VMEM((cx, cy, cz), f32),
-            pltpu.VMEM((SUBSTEPS - 1, cx + 2 * H, cy + 2 * R, cz), f32),
+            pltpu.VMEM((cx + 2 * R, cy + 2 * R, cz), f32),
+            pltpu.VMEM((cx + 2 * H, cy + 2 * R, cz), f32),
             pltpu.VMEM((cx, cy, cz), f32),
             pltpu.VMEM((cx, cy, cz), f32),
-            pltpu.VMEM((SUBSTEPS + 1, 2, cy, cz), f32),
-            pltpu.VMEM((SUBSTEPS + 1, 2, 3, cy + 2 * R, cz), f32),
+            pltpu.VMEM((4, 2, cy, cz), f32),
+            pltpu.VMEM((4, 2, 3, cy + 2 * R, cz), f32),
             pltpu.VMEM((2, cy + 2 * R, cz), f32),
-            pltpu.VMEM((SUBSTEPS - 1, 2, cx // 2, 2 * H, cz), f32),
-            pltpu.VMEM((SUBSTEPS - 1, 2, cx // 2, 2 * H, cz), f32),
+            pltpu.VMEM((2, H, cy, cz), f32),
+            pltpu.VMEM((2, cx // 2, 2 * H, cz), f32),
+            pltpu.VMEM((2, cx // 2, 2 * H, cz), f32),
             pltpu.VMEM((3, 2 * cz, 2 * cz), jnp.bfloat16),
             pltpu.VMEM((2, 2, 4 * cz, 2 * cz), jnp.bfloat16),
             pltpu.VMEM((cy, cz), f32),
-            pltpu.VMEM((2 * (6 * cy + 12 * R) + 2 * (SUBSTEPS - 1) * cy, cz), f32),
+            pltpu.VMEM((2 * (6 * cy + 12 * R) + 8 * cy + 4 * R, cz), f32),
             pltpu.VMEM((spare_rows, cz), f32),
             pltpu.VMEM((cx, cy, cz), f32),
             pltpu.SMEM(weights.shape, f32),
             pltpu.VMEM((summed, 1, cz), f32),
             pltpu.VMEM((ny, 1, cz), f32),
             pltpu.SemaphoreType.DMA((len(FLAT) + 1,)),
-            pltpu.SemaphoreType.DMA((2, len(FLAT) + 1 + SUBSTEPS // 2)),
+            pltpu.SemaphoreType.DMA((2, len(FLAT) + 2)),
             pltpu.SemaphoreType.DMA((stages, most)),
             pltpu.SemaphoreType.DMA((stages, most)),
             pltpu.SemaphoreType.DMA((3,)),

time: 29.9 us -> 28.9 us (0.967)
  Pallas kernels: 29.1 us -> 28.2 us
    pallas_call x1, Pallas kernels: 28.3 us -> 27.3 us  [shards(): pl.pallas_call(functools.partial(kernel, sizes), out_shape=(jax.ShapeDtyp...]
where the time goes in v6:
time: 28.9 us; the launch traced here: 28.8 us
  Pallas kernels  28.2 us (98%)
  between operations  0.64 us (2%)
    pallas_call x1, Pallas kernels, shards(): pl.pallas_call(functools.partial(kernel, sizes), out_shape=(jax.ShapeDtyp...  27.3 us
    pallas_call x1, Pallas kernels, shards(): pl.pallas_call(finish, out_shape=(jax.ShapeDtypeStruct(wave.shape, f32),...  0.81 us

profile of v6, /device:TPU:0, one launch (start us, length us, event | category | flops | bytes accessed | tf_op | source)
XLA Modules:
  0.0 28.8 jit_solution(6625686687386583631)
XLA Ops:
  0.6 27.3 %shard_map.50 = (f32[16,32,128]{2,1,0:T(8,128)S(1)}, f32[16,32,128]{2,1,0:T(8,128)S(1)}, f32[8,128]{1,0:T(8,128)S(1)}) custom-call(f32[3,17]{1,0:T(4,128)} %w_hbm.1, f32[16,32,128]{2,1,0:T(8,128)} %wave_hbm.1, f32[16,32,128]{2,1,0:T(8,128)} %ext_hbm.1), custom_call_target="tpu_custom_call" | custom-call | tf_op jit(solution)/shard_map/pallas_call | solution.py:634
  28.0 0.8 %shard_map.51 = (f32[16,32,128]{2,1,0:T(8,128)}, f32[16,32,128]{2,1,0:T(8,128)}) custom-call(f32[16,32,128]{2,1,0:T(8,128)S(1)} %get-tuple-element.5.psi_ref, f32[16,32,128]{2,1,0:T(8,128)S(1)} %get-tuple-element.6.corr_ref, f32[8,128]{1,0:T(8,128)S(1)} %get-tuple-element.7.scale_ref), custom_call_target="tpu_custom_call" | custom-call | tf_op jit(solution)/shard_map/pallas_call | solution.py:673

commit v7 on v6

--- a/solution.py
+++ b/solution.py
@@ -35,7 +35,7 @@
 
 
 def kernel(sizes, w_hbm, wave_hbm, ext_hbm, out_ref, corr_ref, scale_ref,
-           wb, sb, yb, co, pb, psi, va, part, pack, zin, zb, vx, ypack, yin, bands, edges, blanks, spill, spare, ext_ref, w_ref,
+           wb, sb, yb, co, pb, psi, va, part, pack, zin, zb, vx, px, ypack, yin, bands, edges, blanks, spill, spare, ext_ref, w_ref,
            sums, sums2, send, recv, send2, recv2, local):
     nx, ny, nz = sizes
     cx, cy, cz = wave_hbm.shape
@@ -421,47 +421,43 @@
     def z_rim(slot, place=1, rows=pl.ds(R, cy)):
         return z_rim_of(*[zin[slot, side, place, rows] for side in range(2)])
 
-    def own_part(buf, reach, weight, first_step):
-        pair = z_rim(0) if first_step else None
+    def y_own(buf, p):
+        up = down = None
+        for k in range(1, H + 1):
+            a = gains[k] * buf[p, pl.ds(R + k, cy - 8)]
+            b = gains[k] * buf[p, pl.ds(R + 8 - k, cy - 8)]
+            up, down = (a, b) if up is None else (up + a, down + b)
+        return jnp.concatenate([up[:8], up[8:] + down[:cy - 16], down[cy - 16:]], 0)
+
+    def y_halo(buf, p, total):
+        low, high = total[:8], total[cy - 8:]
+        for k in range(1, H + 1):
+            low = low + gains[k] * buf[p, pl.ds(R - k, 8)]
+            high = high + gains[k] * buf[p, pl.ds(R + cy - 8 + k, 8)]
+        return jnp.concatenate([low, total[8:cy - 8], high], 0)
+
+    def advance(buf, reach, weight, pair, put):
         own = pl.ds(R, cy)
         step = 2 * GROUP
         for g in range(0, cx, step):
             along = dot(planes(buf, reach + g, step, own), bands[2])
             for i in range(g, g + step):
                 total = buf[reach + i, own] * weight(i) + along[(i - g) * cy:(i - g + 1) * cy]
-                if first_step:
-                    total = total + from_rim(pair, i, H)
                 for k in range(1, H + 1):
-                    pairs = [buf[reach + j, own] for j in (i - k, i + k) if first_step or 0 <= j < cx]
-                    if first_step:
+                    pairs = [buf[reach + j, own] for j in (i - k, i + k) if pair is not None or 0 <= j < cx]
+                    if pair is not None:
                         pairs += [buf[reach + i, pl.ds(R + j, cy)] for j in (-k, k)]
                     both = pairs[0]
                     for p in pairs[1:]:
                         both = both + p
                     total = total + gains[k] * both
-                if not first_step:
-                    up = down = None
-                    for k in range(1, H + 1):
-                        a = gains[k] * buf[reach + i, pl.ds(R + k, cy - 8)]
-                        b = gains[k] * buf[reach + i, pl.ds(R + 8 - k, cy - 8)]
-                        up, down = (a, b) if up is None else (up + a, down + b)
-                    total = total + jnp.concatenate([up[:8], up[8:] + down[:cy - 16], down[cy - 16:]], 0)
-                part[i] = total
-
-    def halo_part(buf, reach, pair, i):
-        total = part[i]
-        for k in range(1, H + 1):
-            for j in (i - k, i + k):
-                if not 0 <= j < cx:
-                    total = total + gains[k] * buf[reach + j, pl.ds(R, cy)]
-        low, high = total[:8], total[cy - 8:]
-        for k in range(1, H + 1):
-            low = low + gains[k] * buf[reach + i, pl.ds(R - k, 8)]
-            high = high + gains[k] * buf[reach + i, pl.ds(R + cy - 8 + k, 8)]
-        return jnp.concatenate([low, total[8:cy - 8], high], 0) + from_rim(pair, i, H)
+                put(i, total + (y_own(buf, reach + i) if pair is None else from_rim(pair, i, H)))
+
+    def keep_part(i, value):
+        part[i] = value
 
     middle = 1.0 + STEP * 0.5 * 3.0 * LAP_COEF[0]
-    own_part(wb, R, lambda i: middle, True)
+    advance(wb, R, lambda i: middle, z_rim(0), keep_part)
     smeared = smear(sb, 1, False, True, src_x, src_z + src_e, src_y + src_xy)
     get_ext.wait()
     psi_packs = va_packs = (zero, zero)
@@ -481,8 +477,7 @@
     pack_out(2, psi_packs)
     pack_out(3, va_packs)
     start(psi_moves)
-    own_part(pb, R, lambda i: va[i], False)
-    arrive(psi_moves)
+    advance(pb, R, lambda i: va[i], None, keep_part)
     own = pl.ds(R, cy)
     inside = {(0, 0): ix > 0, (0, 1): ix < nx - 1, (1, 0): iy > 0, (1, 1): iy < ny - 1, (2, 0): iz > 0, (2, 1): iz < nz - 1}
 
@@ -497,29 +492,7 @@
             total = gains[k] * pairs if total is None else total + gains[k] * pairs
         return total
 
-    for side in range(2):
-        pair = z_rim(2, 2 * side)
-        begin = cx if side else -H
-        along = dot(planes(pb, R + begin, H, own), bands[2])
-        for n in range(H):
-            p = begin + n
-            total = pb[R + p, own] * vx[side, n] + along[n * cy:(n + 1) * cy] + star(p, R, cy)
-            psi[H + p, own] = kept(0, side, total + from_rim(pair, p % cx, H))
-    for side in range(2):
-        first = R + cy - H if side else R - H
-        pair = z_rim(2, 1, pl.ds(first, 2 * H))
-        centers = [pb[R + i, pl.ds(first, 2 * H)] for i in range(cx)]
-        along = dot(jnp.concatenate(centers, 0), bands[2])
-        for i in range(cx):
-            weight = yin[side, i // 2]
-            if i % 2 != side:
-                weight = pltpu.roll(weight, H, 0)
-            total = centers[i] * weight + along[i * 2 * H:(i + 1) * 2 * H] + star(i, first, 2 * H)
-            total = kept(1, side, total + from_rim(pair, i, H))
-            if side:
-                psi[H + i, pl.ds(R + cy, H)] = total[H:]
-            else:
-                psi[H + i, pl.ds(R - H, H)] = total[:H]
+    arrive(psi_z)
     rim = []
     cell = lax.rem(at, per)
     for side in range(2):
@@ -539,17 +512,55 @@
             pairs += zin[2, side, 1, pl.ds(R - k, cy)] + zin[2, side, 1, pl.ds(R + k, cy)]
             total = total + gains[k] * pairs
         rim.append(kept(2, side, total))
+    arrive(psi_x)
     pair = z_rim(2)
     for i in range(cx):
-        psi[H + i, own] = halo_part(pb, R, pair, i)
-    own_part(psi, H, lambda i: va[i], False)
-    pair = z_rim_of(*rim)
-    total = zero
+        total = part[i] + from_rim(pair, i, H)
+        for k in range(1, H + 1):
+            for j in (i - k, i + k):
+                if not 0 <= j < cx:
+                    total = total + gains[k] * pb[R + j, own]
+        part[i] = total
+    for side in range(2):
+        pair = z_rim(2, 2 * side)
+        begin = cx if side else -H
+        along = dot(planes(pb, R + begin, H, own), bands[2])
+        for n in range(H):
+            p = begin + n
+            total = pb[R + p, own] * vx[side, n] + along[n * cy:(n + 1) * cy]
+            for k in range(1, H + 1):
+                total = total + gains[k] * (pb[R + p - k, own] + pb[R + p + k, own])
+            px[side, n] = total + y_own(pb, R + p) + from_rim(pair, p % cx, H)
+    arrive(psi_y)
+    for side in range(2):
+        first = R + cy - H if side else R - H
+        pair = z_rim(2, 1, pl.ds(first, 2 * H))
+        centers = [pb[R + i, pl.ds(first, 2 * H)] for i in range(cx)]
+        along = dot(jnp.concatenate(centers, 0), bands[2])
+        for i in range(cx):
+            weight = yin[side, i // 2]
+            if i % 2 != side:
+                weight = pltpu.roll(weight, H, 0)
+            total = centers[i] * weight + along[i * 2 * H:(i + 1) * 2 * H] + star(i, first, 2 * H)
+            total = kept(1, side, total + from_rim(pair, i, H))
+            if side:
+                psi[H + i, pl.ds(R + cy, H)] = total[H:]
+            else:
+                psi[H + i, pl.ds(R - H, H)] = total[:H]
+    for side in range(2):
+        begin = cx if side else -H
+        for n in range(H):
+            psi[H + begin + n, own] = kept(0, side, y_halo(pb, R + begin + n, px[side, n]))
     for i in range(cx):
-        value = halo_part(psi, H, pair, i)
+        psi[H + i, own] = y_halo(pb, R + i, part[i])
+    totals = [zero]
+
+    def finish_cell(i, value):
         out_ref[i] = value
-        total = total + value * value
-
+        totals[0] = totals[0] + value * value
+
+    advance(psi, H, lambda i: va[i], z_rim_of(*rim), finish_cell)
+    total = totals[0]
     partial = jnp.sum(total, axis=0, keepdims=True)
     def all_sum(value, slots, ssem, rsem, me, n, ids):
         if n == 1:
@@ -650,6 +661,7 @@
             pltpu.VMEM((4, 2, 3, cy + 2 * R, cz), f32),
             pltpu.VMEM((2, cy + 2 * R, cz), f32),
             pltpu.VMEM((2, H, cy, cz), f32),
+            pltpu.VMEM((2, H, cy, cz), f32),
             pltpu.VMEM((2, cx // 2, 2 * H, cz), f32),
             pltpu.VMEM((2, cx // 2, 2 * H, cz), f32),
             pltpu.VMEM((3, 2 * cz, 2 * cz), jnp.bfloat16),

time: 28.9 us -> 28.6 us (0.990)
  Pallas kernels: 28.2 us -> 27.8 us
    pallas_call x1, Pallas kernels: 27.3 us -> 27 us  [shards(): pl.pallas_call(functools.partial(kernel, sizes), out_shape=(jax.ShapeDtyp...]
where the time goes in v7:
time: 28.6 us; the launch traced here: 28.4 us
  Pallas kernels  27.8 us (97%)
  between operations  0.64 us (2%)
    pallas_call x1, Pallas kernels, shards(): pl.pallas_call(functools.partial(kernel, sizes), out_shape=(jax.ShapeDtyp...  27 us
    pallas_call x1, Pallas kernels, shards(): pl.pallas_call(finish, out_shape=(jax.ShapeDtypeStruct(wave.shape, f32),...  0.81 us

profile of v7, /device:TPU:0, one launch (start us, length us, event | category | flops | bytes accessed | tf_op | source)
XLA Modules:
  0.0 28.4 jit_solution(17679932928449974286)
XLA Ops:
  0.6 27.0 %shard_map.50 = (f32[16,32,128]{2,1,0:T(8,128)S(1)}, f32[16,32,128]{2,1,0:T(8,128)S(1)}, f32[8,128]{1,0:T(8,128)S(1)}) custom-call(f32[3,17]{1,0:T(4,128)} %w_hbm.1, f32[16,32,128]{2,1,0:T(8,128)} %wave_hbm.1, f32[16,32,128]{2,1,0:T(8,128)} %ext_hbm.1), custom_call_target="tpu_custom_call" | custom-call | tf_op jit(solution)/shard_map/pallas_call | solution.py:645
  27.6 0.8 %shard_map.51 = (f32[16,32,128]{2,1,0:T(8,128)}, f32[16,32,128]{2,1,0:T(8,128)}) custom-call(f32[16,32,128]{2,1,0:T(8,128)S(1)} %get-tuple-element.5.psi_ref, f32[16,32,128]{2,1,0:T(8,128)S(1)} %get-tuple-element.6.corr_ref, f32[8,128]{1,0:T(8,128)S(1)} %get-tuple-element.7.scale_ref), custom_call_target="tpu_custom_call" | custom-call | tf_op jit(solution)/shard_map/pallas_call | solution.py:685

commit v8 on v7

--- a/solution.py
+++ b/solution.py
@@ -194,7 +194,7 @@
                 out.append(message(pack.at[slot, 0, rows], zin.at[slot, 1, 1 - dx, into], dx, dy, -1, group))
         return out
 
-    def side_messages(src, dst, moves, group, part=0, parts=1, wide=R):
+    def side_messages(src, dst, moves, group, part=0, parts=1, wide=R, tall=R):
         out = []
         for dx, dy in moves:
             if dx > 0:
@@ -205,9 +205,9 @@
                 some = cx // parts
                 sx, tx = pl.ds(part * some, some), pl.ds(R + part * some, some)
             if dy > 0:
-                sy, ty = pl.ds(cy - R, R), pl.ds(0, R)
+                sy, ty = pl.ds(cy - tall, tall), pl.ds(R - tall, tall)
             elif dy < 0:
-                sy, ty = pl.ds(0, R), pl.ds(R + cy, R)
+                sy, ty = pl.ds(0, tall), pl.ds(R + cy, tall)
             else:
                 some = cy // parts
                 sy, ty = pl.ds(part * some, some), pl.ds(R + part * some, some)
@@ -233,7 +233,7 @@
     psi_y = side_messages(own_psi, pb, face_y, 2) + [
         message(ypack.at[1], yin.at[0], 0, 1, 0, 2),
         message(ypack.at[0], yin.at[1], 0, -1, 0, 2),
-    ] + side_messages(own_psi, pb, edge_xy, 2, wide=H)
+    ] + side_messages(own_psi, pb, edge_xy, 2, wide=H, tall=H)
     psi_z = z_messages(2, (-1, 0, 1), (0,), 2) + z_messages(2, (0,), (-1, 1), 2) + z_messages(3, (0,), (0,), 2)
     psi_moves = psi_z + psi_x + psi_y
 

time: 28.6 us -> 28.5 us (level)
  no operation moved by 1% of the time
where the time goes in v8:
time: 28.5 us; the launch traced here: 28.4 us
  Pallas kernels  27.7 us (97%)
  between operations  0.64 us (2%)
    pallas_call x1, Pallas kernels, shards(): pl.pallas_call(functools.partial(kernel, sizes), out_shape=(jax.ShapeDtyp...  26.9 us
    pallas_call x1, Pallas kernels, shards(): pl.pallas_call(finish, out_shape=(jax.ShapeDtypeStruct(wave.shape, f32),...  0.81 us

profile of v8, /device:TPU:0, one launch (start us, length us, event | category | flops | bytes accessed | tf_op | source)
XLA Modules:
  0.0 28.4 jit_solution(5242455894183850840)
XLA Ops:
  0.6 26.9 %shard_map.50 = (f32[16,32,128]{2,1,0:T(8,128)S(1)}, f32[16,32,128]{2,1,0:T(8,128)S(1)}, f32[8,128]{1,0:T(8,128)S(1)}) custom-call(f32[3,17]{1,0:T(4,128)} %w_hbm.1, f32[16,32,128]{2,1,0:T(8,128)} %wave_hbm.1, f32[16,32,128]{2,1,0:T(8,128)} %ext_hbm.1), custom_call_target="tpu_custom_call" | custom-call | tf_op jit(solution)/shard_map/pallas_call | solution.py:645
  27.6 0.8 %shard_map.51 = (f32[16,32,128]{2,1,0:T(8,128)}, f32[16,32,128]{2,1,0:T(8,128)}) custom-call(f32[16,32,128]{2,1,0:T(8,128)S(1)} %get-tuple-element.5.psi_ref, f32[16,32,128]{2,1,0:T(8,128)S(1)} %get-tuple-element.6.corr_ref, f32[8,128]{1,0:T(8,128)S(1)} %get-tuple-element.7.scale_ref), custom_call_target="tpu_custom_call" | custom-call | tf_op jit(solution)/shard_map/pallas_call | solution.py:685
